TPU v7x, 256 devices: a whole 4x4x8 slice. The times are simulated.
256 devices in a mesh: dp: 32 (over z, y), block: 8 (over x, core).
Axes of the slice: x: 4, y: 4, z: 8, core: 2. Of those that a mesh axis runs over, the one named last changes fastest.
Arguments:
- x_act: bfloat16 [8, 16384, 4096], P('block', 'dp')
- g_out: bfloat16 [8, 16384, 4096], P('block', 'dp')
- proj_in: bfloat16 [8, 4096, 64], P('block'), may hold values from -0.09375 to 0.09375
- proj_out: bfloat16 [8, 4096, 64], P('block'), may hold values from -0.09375 to 0.09375
- queries: bfloat16 [8, 2048, 4096], P('block', 'dp'), may hold values from -6 to 6
- cand_ids: int32 [32, 32, 2], P('dp'), may hold values from 0 to 15, as said below
- cand_counts: int32 [32, 32], P('dp'), may hold values from 0 to 2, as said below
Outputs:
- scores: float32 [2048, 128], P(('dp', 'block'))
Inputs may be any that keep to these rules, and one draw needn't show every extreme that they name: `cand_ids`: each list of a training shard d for an owner p names 2 distinct query blocks of p; slots at or past cand_counts[d, p] are padding. Every training shard d has cand_counts[d, d] = 2.
All inputs are finite; a program needn't handle non-finite values.
Results may differ from a plain program's by a relative error of at most 0.0096.
Values may be sent and summed in bfloat16 or wider, within the bound.
No kernel may reach another device: no remote copies, remote signals or barrier semaphores. Data moves between devices by JAX's collectives and lax.ppermute only.
A program may use at most 64 MiB of HBM per device.

v0:
```python
import jax
import jax.numpy as jnp
from jax import lax
from jax.sharding import PartitionSpec as P

E_DEV = 4
SEQ = 128
QB = 4
CAP = 2


DAMP = 0.1


def kron_inverse(factor):
    width = factor.shape[0]
    identity = jnp.eye(width, dtype=jnp.float32)
    damping = DAMP * jnp.trace(factor) / width + 1e-06
    lower_factor = jnp.linalg.cholesky(factor + damping * identity)
    return jax.scipy.linalg.cho_solve((lower_factor, True), identity)


def body(x_act, g_out, proj_in, proj_out, queries, cand_ids, cand_counts):
    act_rows = x_act[0]
    grad_rows = g_out[0]
    row_count = act_rows.shape[0]
    width = proj_in.shape[2]
    n_owners = lax.axis_size("dp")
    n_layers = lax.axis_size("block")
    act_proj = jnp.dot(act_rows, proj_in[0], preferred_element_type=jnp.float32).astype(
        jnp.bfloat16
    )
    grad_proj = jnp.dot(grad_rows, proj_out[0], preferred_element_type=jnp.float32).astype(
        jnp.bfloat16
    )
    contract_rows = (((0,), (0,)), ((), ()))
    part_a = lax.dot_general(act_proj, act_proj, contract_rows, preferred_element_type=jnp.float32)
    part_g = lax.dot_general(
        grad_proj, grad_proj, contract_rows, preferred_element_type=jnp.float32
    )
    factor_a, factor_g = lax.psum((part_a, part_g), "dp")
    token_total = row_count * n_owners
    inverse_a = kron_inverse(factor_a / token_total)
    inverse_g = kron_inverse(factor_g / token_total)
    act_three = act_proj.reshape(E_DEV, SEQ, width)
    grad_three = grad_proj.reshape(E_DEV, SEQ, width)
    example_grad = (
        jnp.einsum("esi,esj->eij", grad_three, act_three, preferred_element_type=jnp.float32) / SEQ
    )
    left_side = jnp.einsum("ij,ejk->eik", inverse_g, example_grad, precision=lax.Precision.HIGHEST)
    precond = jnp.einsum("eik,kl->eil", left_side, inverse_a, precision=lax.Precision.HIGHEST)
    precond = precond.reshape(E_DEV, width * width).astype(jnp.bfloat16)
    req_ids, req_counts = (
        lax.all_to_all(cand_ids, "dp", split_axis=1, concat_axis=0, tiled=True),
        lax.all_to_all(cand_counts, "dp", split_axis=1, concat_axis=0, tiled=True),
    )
    req_ids = req_ids.reshape(n_owners, CAP)
    req_counts = req_counts.reshape(n_owners)
    query_rows = queries[0]
    owned = query_rows.shape[0]
    block_count = owned // QB
    slot_live = jnp.arange(CAP)[None, :] < req_counts[:, None]
    onehot = (
        (req_ids[:, :, None] == jnp.arange(block_count)[None, None, :]) & slot_live[:, :, None]
    ).astype(jnp.float32)
    dense_part = lax.dot_general(
        query_rows,
        lax.all_gather(precond, "dp", axis=0, tiled=True),
        (((1,), (1,)), ((), ())),
        preferred_element_type=jnp.float32,
    )
    live_blocks = jnp.sum(onehot, axis=1)
    mask_full = jnp.broadcast_to(
        jnp.transpose(live_blocks)[:, None, :, None], (block_count, QB, n_owners, E_DEV)
    ).reshape(owned, n_owners * E_DEV)
    layer_part = dense_part * mask_full
    scale = 1.0 / float(width * width * n_layers) ** 0.5
    return lax.psum_scatter(layer_part * scale, "block", scatter_dimension=0, tiled=True)


def solution(mesh):
    return jax.shard_map(
        body,
        mesh=mesh,
        in_specs=(
            P("block", "dp", None),
            P("block", "dp", None),
            P("block", None, None),
            P("block", None, None),
            P("block", "dp", None),
            P("dp", None, None),
            P("dp", None),
        ),
        out_specs=P(("dp", "block"), None),
        check_vma=False,
    )
```

profile of v0, /device:TPU:1, one launch (start us, length us, event | category | flops | bytes accessed | tf_op | source)
XLA Modules:
  0.0 290.4 jit_solution(2975817334751202043)
XLA Ops:
  6.5 1.0 copy-done
  7.6 3.7 %fusion.4 = bf16[512,64]{0,1:T(8,128)(2,1)S(1)} fusion(bf16[1,512,4096]{2,1,0:T(8,128)(2,1)} %param.11, bf16[1,4096,64]{1,2,0:T(8,128)(2,1)S(1)} %copy-done), kind=kOutput, calls=%fused_computation.6 | convolution fusion | flops 268468224 | bytes 4784128 | tf_op jit(solution)/shard_map/dot_general | solution.py:33
  11.5 1.4 fusion.7
  13.2 118.9 %all-reduce.1 = (f32[64,64]{0,1:T(8,128)S(1)}, f32[64,64]{0,1:T(8,128)S(1)}) all-reduce(f32[64,64]{0,1:T(8,128)S(1)} %fusion.32, f32[64,64]{0,1:T(8,128)S(1)} %fusion.33), channel_id=1, replica_groups=mesh['dp'=32,'block'=8] {'dp'}, use_global_device_ids=true, to_apply=%region_0.0 | all-reduce | flops 8192 | bytes 65536 | tf_op jit(solution)/shard_map/psum | solution.py:41
  132.2 0.7 select_reduce_fusion.3
  134.9 5.8 %cholesky.55 = f32[64,64]{1,0:T(8,128)S(1)} custom-call(f32[64,64]{1,0:T(8,128)S(1)} %fusion.27), custom_call_target="Cholesky" | custom-call | tf_op jit(solution)/shard_map/jit(cholesky)/cholesky | solution.py:19
  140.8 0.6 compare_reduce_fusion
  141.5 0.7 fusion.24
  142.1 4.9 %custom-call.9 = f32[1,64,64]{1,2,0:T(8,128)S(1)} custom-call(f32[1,64,64]{2,1,0:T(8,128)S(1)} %fusion.24), custom_call_target="InvertDiagBlocksLowerTriangular" | custom-call | tf_op jit(solution)/shard_map/jit(_cho_solve)/triangular_solve | solution.py:20
  147.5 5.8 %cholesky.44 = f32[64,64]{1,0:T(8,128)S(1)} custom-call(f32[64,64]{1,0:T(8,128)S(1)} %fusion.30), custom_call_target="Cholesky" | custom-call | tf_op jit(solution)/shard_map/jit(cholesky)/cholesky | solution.py:19
  154.1 0.7 fusion.23
  154.7 4.9 %custom-call.8 = f32[1,64,64]{1,2,0:T(8,128)S(1)} custom-call(f32[1,64,64]{2,1,0:T(8,128)S(1)} %fusion.23), custom_call_target="InvertDiagBlocksLowerTriangular" | custom-call | tf_op jit(solution)/shard_map/jit(_cho_solve)/triangular_solve | solution.py:20
  160.8 0.7 reshape.60
  161.6 0.7 copy.52
  162.3 3.8 %all-to-all-start.1 = ((s32[1,32,1]{2,0,1:T(1,128)}), s32[1,32,1]{2,0,1:T(1,128)S(1)}, u32[]{:S(2)}, u32[]{:S(2)}) async-start(s32[1,32,1]{2,0,1:T(1,128)} %copy.52), calls=%async_computation.1 | async-start | bytes 32768 | tf_op jit(solution)/shard_map/all_to_all | solution.py:55
  166.1 0.7 copy.50
  168.1 6.6 %all-to-all-done.1 = s32[1,32,1]{2,0,1:T(1,128)S(1)} async-done(((s32[1,32,1]{2,0,1:T(1,128)}), s32[1,32,1]{2,0,1:T(1,128)S(1)}, u32[]{:S(2)}, u32[]{:S(2)}) %all-to-all-start.1) | async-done | bytes 160 | tf_op jit(solution)/shard_map/all_to_all | solution.py:55
  174.7 3.8 %all-to-all-start = ((s32[1,32,2]{2,0,1:T(1,128)}), s32[1,32,2]{2,0,1:T(1,128)S(1)}, u32[]{:S(2)}, u32[]{:S(2)}) async-start(s32[1,32,2]{2,0,1:T(1,128)} %copy.50), calls=%async_computation | async-start | bytes 32768 | tf_op jit(solution)/shard_map/all_to_all | solution.py:54
  178.5 0.7 reduce.4
  179.2 7.8 %all-to-all-done = s32[1,32,2]{2,0,1:T(1,128)S(1)} async-done(((s32[1,32,2]{2,0,1:T(1,128)}), s32[1,32,2]{2,0,1:T(1,128)S(1)}, u32[]{:S(2)}, u32[]{:S(2)}) %all-to-all-start) | async-done | bytes 288 | tf_op jit(solution)/shard_map/all_to_all | solution.py:54
  187.2 0.6 reshape.59
  187.9 68.2 %all-gather.3.cloned.1.call-done = bf16[32,4,4096]{2,1,0:T(4,128)(2,1)} async-done(((bf16[1,4,4096]{2,1,0:T(4,128)(2,1)}), bf16[32,4,4096]{2,1,0:T(4,128)(2,1)}) %all-gather.3.cloned.1.call-update) | async-done | bytes 1048592 | tf_op jit(solution)/shard_map/all_gather | solution.py:68
  256.0 1.3 reshape.61
  257.9 25.1 %all-reduce = f32[64,128]{1,0:T(8,128)S(1)} all-reduce(f32[64,128]{1,0:T(8,128)S(1)} %fusion.11), channel_id=2, replica_groups=mesh['dp'=32,'block'=8] {'block'}, use_global_device_ids=true, to_apply=%region_7.10.clone | all-reduce | flops 8192 | bytes 65536
  (40 shorter events, 5.5 us)
Async XLA Ops:
  6.5 1.0 copy-start
  6.5 5.0 %copy-start.2 = (bf16[1,4096,64]{1,2,0:T(8,128)(2,1)S(1)}, bf16[1,4096,64]{1,2,0:T(8,128)(2,1)}, u32[]{:S(2)}) copy-start(bf16[1,4096,64]{1,2,0:T(8,128)(2,1)} %param.12) | copy-start | bytes 1572868
  6.5 249.5 %all-gather.3.cloned.1.call-start = ((), (), s32[]{:S(2)}) async-start(), calls=%async_computation.2 | async-start | bytes 1081344 | tf_op jit(solution)/shard_map/all_gather | solution.py:68
  7.6 3.9 %copy-start.1 = (bf16[1,512,4096]{2,1,0:T(8,128)(2,1)S(1)}, bf16[1,512,4096]{2,1,0:T(8,128)(2,1)}, u32[]{:S(2)}) copy-start(bf16[1,512,4096]{2,1,0:T(8,128)(2,1)} %param.10) | copy-start | bytes 12582916
  11.3 150.3 %copy-start.5 = (s32[1,32]{1,0:T(1,128)S(1)}, s32[1,32]{1,0:T(1,128)}, u32[]{:S(2)}) copy-start(s32[1,32]{1,0:T(1,128)} %param.16) | copy-start | bytes 388
  11.3 154.8 %copy-start.4 = (s32[1,32,2]{1,2,0:T(2,128)S(1)}, s32[1,32,2]{1,2,0:T(2,128)}, u32[]{:S(2)}) copy-start(s32[1,32,2]{1,2,0:T(2,128)} %param.15) | copy-start | bytes 772
  11.3 155.5 %copy-start.6 = (u32[256]{0:T(256)S(1)}, u32[256]{0:T(256)}, u32[]{:S(2)}) copy-start(u32[256]{0:T(256)} %constant.72) | copy-start | bytes 3076
  12.9 244.5 %copy-start.3 = (bf16[1,64,4096]{2,1,0:T(8,128)(2,1)S(1)}, bf16[1,64,4096]{2,1,0:T(8,128)(2,1)}, u32[]{:S(2)}) copy-start(bf16[1,64,4096]{2,1,0:T(8,128)(2,1)} %param.14) | copy-start | bytes 1572868
  162.3 12.4 %all-to-all-start.1 = ((s32[1,32,1]{2,0,1:T(1,128)}), s32[1,32,1]{2,0,1:T(1,128)S(1)}, u32[]{:S(2)}, u32[]{:S(2)}) async-start(s32[1,32,1]{2,0,1:T(1,128)} %copy.52), calls=%async_computation.1 | async-start | bytes 32768 | tf_op jit(solution)/shard_map/all_to_all | solution.py:55
  174.7 12.2 %all-to-all-start = ((s32[1,32,2]{2,0,1:T(1,128)}), s32[1,32,2]{2,0,1:T(1,128)S(1)}, u32[]{:S(2)}, u32[]{:S(2)}) async-start(s32[1,32,2]{2,0,1:T(1,128)} %copy.50), calls=%async_computation | async-start | bytes 32768 | tf_op jit(solution)/shard_map/all_to_all | solution.py:54
Sparse Core Ops, SparseCore 0:
  161.7 94.2 all-gather.2
where the time goes:
time: 292 us; the launch traced here: 290 us
  blocking collectives  144 us (49%)
  waiting for transfers between devices  82.6 us (28%)
  other arithmetic  26.1 us (9%)
  between operations  15.6 us (5%)
  starting transfers between devices  7.64 us (3%)
  matrix products  7.64 us (3%)
  local copies, waits for them, and re-layouts  6.72 us (2%)
    psum x1, blocking collectives, body(): factor_a, factor_g = lax.psum((part_a, part_g), 'dp')  119 us
    all_gather x1, waiting for transfers between devices, body(): lax.all_gather(precond, 'dp', axis=0, tiled=True)  68.2 us
    unnamed x1, blocking collectives  25.1 us
    another operation x6, other arithmetic, kron_inverse(): lower_factor = jnp.linalg.cholesky(factor + damping * identity)  13 us
    another operation x4, other arithmetic, kron_inverse(): return jax.scipy.linalg.cho_solve((lower_factor, True), identity)  11.1 us
    all_to_all x1, waiting for transfers between devices, body(): lax.all_to_all(cand_ids, 'dp', split_axis=1, concat_axis=0, tiled=True)  7.76 us
    all_to_all x1, waiting for transfers between devices, body(): lax.all_to_all(cand_counts, 'dp', split_axis=1, concat_axis=0, tiled=True)  6.65 us
  transfers between devices with their start and end apart: 3, of which 3 were waited for; matrix products, arithmetic and copies ran while one was open for 1% of the time, Pallas kernels for 0%

commit v1 on v0

v1 whole, which is shorter than its diff:
```python
import jax
import jax.numpy as jnp
from jax import lax
from jax.sharding import PartitionSpec as P

E_DEV = 4
SEQ = 128
QB = 4
CAP = 2
Z = 8
Y = 4
F16 = jnp.float16
F32 = jnp.float32
BF16 = jnp.bfloat16
DAMP = 0.1
HI = lax.Precision.HIGHEST

Z_GROUPS = [[z * Y + y for z in range(Z)] for y in range(Y)]
Y_GROUPS = [[z * Y + y for y in range(Y)] for z in range(Z)]


def y_shift(k):
    return [(z * Y + y, z * Y + (y + k) % Y) for z in range(Z) for y in range(Y)]


def spread(x, n):
    return jnp.broadcast_to(x[None], (n,) + x.shape)


def exponent(m):
    return jnp.clip(jnp.floor(jnp.log2(jnp.maximum(m, 1e-30))), -96.0, 96.0)


def kron_inverse(factor):
    width = factor.shape[0]
    identity = jnp.eye(width, dtype=F32)
    damping = DAMP * jnp.trace(factor) / width + 1e-06
    lower_factor = jnp.linalg.cholesky(factor + damping * identity)
    return jax.scipy.linalg.cho_solve((lower_factor, True), identity)


def body(x_act, g_out, proj_in, proj_out, queries, cand_ids, cand_counts):
    width = proj_in.shape[2]
    n_owners = lax.axis_size("dp")
    n_layers = lax.axis_size("block")
    me = lax.axis_index("dp")
    my_y = me % Y
    act = jnp.dot(x_act[0], proj_in[0], preferred_element_type=F32).astype(BF16)
    grad = jnp.dot(g_out[0], proj_out[0], preferred_element_type=F32).astype(BF16)
    rows = (((0,), (0,)), ((), ()))
    part_a = lax.dot_general(act, act, rows, preferred_element_type=F32)
    part_g = lax.dot_general(grad, grad, rows, preferred_element_type=F32)
    example = jnp.einsum(
        "esi,esj->eij",
        grad.reshape(E_DEV, SEQ, width),
        act.reshape(E_DEV, SEQ, width),
        preferred_element_type=F32,
    ) / SEQ

    e_exp = exponent(jnp.max(jnp.abs(example), axis=(1, 2)))
    small = (example * (4096.0 * jnp.exp2(-e_exp))[:, None, None]).astype(F16)
    small = small.reshape(128, 128)
    a_exp = exponent(jnp.max(jnp.diagonal(part_a)))
    g_exp = exponent(jnp.max(jnp.diagonal(part_g)))
    parts = jnp.concatenate(
        [part_a * (256.0 * jnp.exp2(-a_exp)), part_g * (256.0 * jnp.exp2(-g_exp))], axis=1
    )
    high = parts.astype(F16)
    low = ((parts - high.astype(F32)) * 2048.0).astype(F16)
    live_slot = jnp.arange(CAP)[None, :] < cand_counts[0][:, None]
    ids = jnp.where(live_slot, cand_ids[0], 99).reshape(n_owners * CAP).astype(F32)
    meta = jnp.concatenate([ids, e_exp, jnp.stack([a_exp, g_exp]), jnp.zeros((58,), F32)])
    meta = jnp.broadcast_to(meta.astype(F16)[None], (16, 128))
    packet = jnp.concatenate([small, meta, high, low], axis=0)

    got = lax.all_to_all(
        spread(packet, Z), "dp", 0, 0, axis_index_groups=Z_GROUPS, tiled=True
    )
    mine = got[:, :144]
    got_meta = got[:, 128, :].astype(F32)
    lane_exp = jnp.where(
        jnp.arange(128)[None, :] < width, got_meta[:, 68:69], got_meta[:, 69:70]
    )
    lane_scale = (jnp.exp2(lane_exp) / 256.0)[:, None, :]
    both = got[:, 144:208].astype(F32) + got[:, 208:272].astype(F32) * (1.0 / 2048.0)
    sums = jnp.sum(both * lane_scale, axis=0)
    sums = jnp.sum(
        lax.all_to_all(spread(sums, Y), "dp", 0, 0, axis_index_groups=Y_GROUPS, tiled=True), axis=0
    )
    token_total = x_act.shape[1] * n_owners
    factors = jnp.stack([sums[:, :width], sums[:, width:]]) / token_total
    inverses = jax.vmap(kron_inverse)(factors)

    gathered = jnp.stack([mine] + [lax.ppermute(mine, "dp", y_shift(k)) for k in range(1, Y)])
    gathered = gathered.reshape(n_owners, 144, 128)
    train = gathered[:, :128].reshape(n_owners * E_DEV, width * width).astype(F32)
    notes = gathered[:, 128].astype(F32)

    query = queries[0].astype(F32).reshape(-1, width, width)
    owned = query.shape[0]
    query = jnp.einsum("qij,jk->qik", query, inverses[0], precision=HI)
    query = jnp.einsum("ij,qjk->qik", inverses[1], query, precision=HI)
    query = query.reshape(owned, width * width)
    dense = lax.dot_general(
        query, train, (((1,), (1,)), ((), ())), precision=HI, preferred_element_type=F32
    )
    slots = lax.dynamic_slice(notes, (0, me * CAP), (n_owners, CAP))
    blocks = (jnp.arange(owned) // QB).astype(F32)
    live = jnp.any(slots[None] == blocks[:, None, None], axis=2)
    scale = 1.0 / float(width * width * n_layers) ** 0.5
    column = jnp.exp2(notes[:, 64:68]) * (scale / 4096.0)
    scores = jnp.where(live[:, :, None], dense.reshape(owned, n_owners, E_DEV) * column[None], 0.0)
    scores = scores.reshape(owned, Y, Z, E_DEV)
    back = jnp.stack([scores[:, (-m) % Y] for m in range(Y)] * 2, axis=1)
    scores = lax.dynamic_slice_in_dim(back, (Y - my_y) % Y, Y, axis=1)
    scores = jnp.swapaxes(scores, 1, 2).reshape(n_layers, owned // n_layers, n_owners * E_DEV)
    return jnp.sum(lax.all_to_all(scores, "block", 0, 0, tiled=True), axis=0)


def solution(mesh):
    return jax.shard_map(
        body,
        mesh=mesh,
        in_specs=(
            P("block", "dp", None),
            P("block", "dp", None),
            P("block", None, None),
            P("block", None, None),
            P("block", "dp", None),
            P("dp", None, None),
            P("dp", None),
        ),
        out_specs=P(("dp", "block"), None),
        check_vma=False,
    )
```

time: 292 us -> 101 us (0.35)
  blocking collectives: 144 us -> 10.7 us
  waiting for transfers between devices: 82.6 us -> 17.6 us
  between operations: 15.6 us -> 1.89 us
  starting transfers between devices: 7.64 us -> 17 us
  local copies, waits for them, and re-layouts: 6.72 us -> 14.4 us
  matrix products: 7.64 us -> 13.3 us
    psum x1 -> x0, blocking collectives: 119 us -> none  [body(): factor_a, factor_g = lax.psum((part_a, part_g), 'dp')]
    all_gather x1 -> x0, waiting for transfers between devices: 68.2 us -> none  [body(): lax.all_gather(precond, 'dp', axis=0, tiled=True)]
    unnamed x1 -> x0, blocking collectives: 25.1 us -> none
    all_to_all x0 -> x1, blocking collectives: none -> 10.7 us  [body(): return jnp.sum(lax.all_to_all(scores, 'block', 0, 0, tiled=True), axis=0)]
    dot_general x8, matrix products: 6.81 us -> 12.8 us  [the longest x1 3.72 us: body(): jnp.dot(g_out[0], proj_out[0], preferred_element_type=F32).astype(BF16)]
    all_to_all x2, starting transfers between devices: 7.64 us -> 13.2 us  [the longest x1 9.02 us: body(): lax.all_to_all(spread(packet, Z), 'dp', 0, 0, axis_index_groups=Z_GROUPS,...]
    ppermute x0 -> x3, starting transfers between devices: none -> 3.83 us  [body(): lax.ppermute(mine, 'dp', y_shift(k))]
    unnamed x19 -> x21, local copies, waits for them, and re-layouts: 4.98 us -> 1.35 us
  transfers between devices with their start and end apart: 3 -> 5, of which waited for: 3 -> 2; matrix products, arithmetic and copies ran while one was open for 1% -> 33% of each run, Pallas kernels for 0% -> 0%
where the time goes in v1:
time: 101 us
  other arithmetic  25.9 us (26%)
  waiting for transfers between devices  17.6 us (17%)
  starting transfers between devices  17 us (17%)
  local copies, waits for them, and re-layouts  14.4 us (14%)
  matrix products  13.3 us (13%)
  blocking collectives  10.7 us (11%)
  between operations  1.89 us (2%)
    all_to_all x1, waiting for transfers between devices, body(): lax.all_to_all(spread(packet, Z), 'dp', 0, 0, axis_index_groups=Z_GROUPS,...  17.4 us
    another operation x4, other arithmetic, kron_inverse(): lower_factor = jnp.linalg.cholesky(factor + damping * identity)  11.9 us
    all_to_all x1, blocking collectives, body(): return jnp.sum(lax.all_to_all(scores, 'block', 0, 0, tiled=True), axis=0)  10.7 us
    another operation x3, other arithmetic, kron_inverse(): return jax.scipy.linalg.cho_solve((lower_factor, True), identity)  9.92 us
    all_to_all x1, starting transfers between devices, body(): lax.all_to_all(spread(packet, Z), 'dp', 0, 0, axis_index_groups=Z_GROUPS,...  9.02 us
    all_to_all x1, starting transfers between devices, body(): lax.all_to_all(spread(sums, Y), 'dp', 0, 0, axis_index_groups=Y_GROUPS, t...  4.19 us
    ppermute x3, starting transfers between devices, body(): lax.ppermute(mine, 'dp', y_shift(k))  3.83 us
    dot_general x1, matrix products, body(): jnp.dot(g_out[0], proj_out[0], preferred_element_type=F32).astype(BF16)  3.72 us
  transfers between devices with their start and end apart: 5, of which 2 were waited for; matrix products, arithmetic and copies ran while one was open for 33% of the time, Pallas kernels for 0%

profile of v1, /device:TPU:1, one launch (start us, length us, event | category | flops | bytes accessed | tf_op | source)
XLA Modules:
  0.0 100.8 jit_solution(4736125792967729793)
XLA Ops:
  0.0 1.0 %copy-done = bf16[1,4096,64]{1,2,0:T(8,128)(2,1)S(1)} copy-done((bf16[1,4096,64]{1,2,0:T(8,128)(2,1)S(1)}, bf16[1,4096,64]{1,2,0:T(8,128)(2,1)}, u32[]{:S(2)}) %copy-start) | copy-done | bytes 524312
  1.0 3.7 %fusion.9 = bf16[512,64]{0,1:T(8,128)(2,1)S(1)} fusion(bf16[1,512,4096]{2,1,0:T(8,128)(2,1)} %param.8, bf16[1,4096,64]{1,2,0:T(8,128)(2,1)S(1)} %copy-done), kind=kOutput, calls=%fused_computation.10 | convolution fusion | flops 268468224 | bytes 4784128 | tf_op jit(solution)/shard_map/dot_general | solution.py:49
  5.0 1.4 %fusion.12 = bf16[512,64]{0,1:T(8,128)(2,1)S(1)} fusion(bf16[1,512,4096]{2,1,0:T(8,128)(2,1)S(1)} %copy-done.1, bf16[1,4096,64]{1,2,0:T(8,128)(2,1)S(1)} %copy-done.2), kind=kOutput, calls=%fused_computation.11 | convolution fusion | flops 268468224 | bytes 4784128 | tf_op jit(solution)/shard_map/dot_general | solution.py:48
  6.8 0.8 gather_fusion
  8.9 0.8 gather_fusion.1
  12.0 0.9 broadcast_in_dim.100
  12.9 9.0 %all-to-all-start = ((f16[8,272,128]{2,1,0:T(8,128)(2,1)}), f16[8,272,128]{2,1,0:T(8,128)(2,1)S(1)}, u32[]{:S(2)}, u32[]{:S(2)}) async-start(f16[8,272,128]{2,1,0:T(8,128)(2,1)} %broadcast_in_dim.100), calls=%async_computation | async-start | bytes 1114112 | tf_op jit(solution)/shard_map/all_to_all | solution.py:76
  21.9 1.1 %reshape.183 = bf16[64,64,64]{2,1,0:T(8,128)(2,1)S(1)} reshape(bf16[1,64,4096]{2,1,0:T(8,128)(2,1)S(1)} %copy-done.3) | data formatting | bytes 1048576 | tf_op jit(solution)/shard_map/reshape | solution.py:99
  23.1 17.4 %all-to-all-done = f16[8,272,128]{2,1,0:T(8,128)(2,1)S(1)} async-done(((f16[8,272,128]{2,1,0:T(8,128)(2,1)}), f16[8,272,128]{2,1,0:T(8,128)(2,1)S(1)}, u32[]{:S(2)}, u32[]{:S(2)}) %all-to-all-start) | async-done | bytes 557088 | tf_op jit(solution)/shard_map/all_to_all | solution.py:76
  40.9 0.6 broadcast_in_dim.107
  41.6 4.2 %all-to-all-start.1 = ((f32[4,64,128]{2,1,0:T(8,128)}), f32[4,64,128]{2,1,0:T(8,128)S(1)}, u32[]{:S(2)}, u32[]{:S(2)}) async-start(f32[4,64,128]{2,1,0:T(8,128)} %broadcast_in_dim.107), calls=%async_computation.1 | async-start | bytes 262144 | tf_op jit(solution)/shard_map/all_to_all | solution.py:88
  45.8 0.8 slice_bitcast_fusion.6
  46.6 2.7 %collective-permute-start.2 = (f16[8,144,128]{2,1,0:T(8,128)(2,1)}, f16[8,144,128]{2,1,0:T(8,128)(2,1)S(1)}, u32[]{:S(2)}, u32[]{:S(2)}) collective-permute-start(f16[8,144,128]{2,1,0:T(8,128)(2,1)} %get-tuple-element.8), channel_id=1, source_target_pairs={{0,24},{8,0},{16,8},{24,16},{32,56},{40,32},{48,40},{56,48},{64,88... | collective-permute-start | bytes 884744 | tf_op jit(solution)/shard_map/ppermute | solution.py:94
  51.1 11.7 %custom-call.11 = f32[2,64,64]{2,1,0:T(8,128)S(1)} custom-call(f32[2,64,64]{2,1,0:T(8,128)S(1)} %fusion.29), custom_call_target="Cholesky" | custom-call | tf_op jit(solution)/shard_map/vmap(jit(cholesky))/cholesky | solution.py:38
  63.0 9.8 %custom-call.12 = f32[2,1,64,64]{2,3,1,0:T(8,128)S(1)} custom-call(f32[2,1,64,64]{3,2,1,0:T(8,128)S(1)} %select_bitcast_fusion), custom_call_target="InvertDiagBlocksLowerTriangular" | custom-call | tf_op jit(solution)/shard_map/vmap(jit(_cho_solve))/triangular_solve | solution.py:39
  73.4 3.1 %fusion.30 = f32[64,64,64]{2,0,1:T(8,128)S(1)} fusion(bf16[64,64,64]{2,1,0:T(8,128)(2,1)S(1)} %reshape.183, f32[2,64,64]{2,1,0:T(8,128)S(1)} %fusion.25), kind=kOutput, calls=%fused_computation.41 | convolution fusion | flops 201326592 | bytes 2129920 | tf_op jit(solution)/shard_map/qij,jk->qik/dot_general | solution.py:101
  76.5 1.8 %fusion.6 = f32[64,64,64]{1,2,0:T(8,128)S(1)} fusion(f32[64,64,64]{2,0,1:T(8,128)S(1)} %fusion.30, f32[2,64,64]{2,1,0:T(8,128)S(1)} %fusion.25), kind=kOutput, calls=%fused_computation.8 | convolution fusion | flops 201326592 | bytes 3178496 | tf_op jit(solution)/shard_map/ij,qjk->qik/dot_general | solution.py:102
  78.3 1.9 %copy.83 = f32[64,64,64]{2,1,0:T(8,128)} copy(f32[64,64,64]{1,2,0:T(8,128)S(1)} %fusion.6) | data formatting | bytes 2097152 | tf_op jit(solution)/shard_map/ij,qjk->qik/transpose | solution.py:102
  80.2 2.1 %reshape.202 = f32[64,4096,1]{1,0,2:T(8,128)S(1)} reshape(f32[64,64,64]{2,1,0:T(8,128)} %copy.83) | data formatting | bytes 2097152 | tf_op jit(solution)/shard_map/reshape | solution.py:103
  82.4 1.4 %pad_maximum_fusion = f16[4,8,144,128]{3,2,1,0:T(8,128)(2,1)S(1)} fusion(f16[1,8,144,128]{3,2,1,0:T(8,128)(2,1)S(1)} %bitcast.96, f16[1,8,144,128]{3,2,1,0:T(8,128)(2,1)S(1)} %bitcast.97, f16[1,8,144,128]{3,2,1,0:T(8,128)(2,1)} %bitcast.9, f16[1,8,144,128]{3,2,1,0:T(8,128)(2,1)S(1)} %get-tuple-element.7), kind=kLoop, calls=%fused_computation.9 | loop fusion | flops 1769472 | bytes 2359296 | tf_op jit(solution)/shard_map/stack | solution.py:94
  83.7 1.3 %slice.99 = f16[32,128,128]{2,1,0:T(8,128)(2,1)} slice(f16[32,144,128]{2,1,0:T(8,128)(2,1)S(1)} %bitcast.94), slice={[0:32], [0:128], [0:128]} | slice | bytes 2097152 | tf_op jit(solution)/shard_map/slice | solution.py:96
  85.0 1.4 %dot_general.36 = f16[32,4,4096]{2,1,0:T(4,128)(2,1)S(1)} reshape(f16[32,128,128]{2,1,0:T(8,128)(2,1)} %slice.99) | data formatting | bytes 2097152 | tf_op jit(solution)/shard_map/dot_general | solution.py:104
  86.7 2.2 %fusion.16 = f32[64,4,8,4]{0,2,1,3:T(8,128)S(1)} fusion(f32[64,4096,1]{1,0,2:T(8,128)S(1)} %reshape.202, f16[32,4,4096]{2,1,0:T(4,128)(2,1)S(1)} %dot_general.36, f32[32,4]{0,1:T(4,128)S(1)} %fusion.35, pred[64,32]{0,1:T(8,128)(4,1)S(1)} %compare_reduce_fusion), kind=kOutput, calls=%fused_computation.14 | convolution fusion | flops 402669568 | bytes 2132480 | tf_op jit(solution)/shard_map/dot_general | solution.py:104
  89.4 10.7 %all_to_all.15 = f32[8,8,128]{2,1,0:T(8,128)S(1)} all-to-all(f32[8,8,128]{2,1,0:T(8,128)S(1)} %copy.89), channel_id=1, replica_groups=mesh['dp'=32,'block'=8] {'block'}, dimensions={0} | all-to-all | bytes 65536 | tf_op jit(solution)/shard_map/all_to_all | solution.py:117
  (77 shorter events, 6.9 us)
Async XLA Ops:
  0.0 1.0 %copy-start = (bf16[1,4096,64]{1,2,0:T(8,128)(2,1)S(1)}, bf16[1,4096,64]{1,2,0:T(8,128)(2,1)}, u32[]{:S(2)}) copy-start(bf16[1,4096,64]{1,2,0:T(8,128)(2,1)} %param.10) | copy-start | bytes 1572868
  1.0 3.9 %copy-start.1 = (bf16[1,512,4096]{2,1,0:T(8,128)(2,1)S(1)}, bf16[1,512,4096]{2,1,0:T(8,128)(2,1)}, u32[]{:S(2)}) copy-start(bf16[1,512,4096]{2,1,0:T(8,128)(2,1)} %param.7) | copy-start | bytes 12582916
  1.0 3.9 %copy-start.2 = (bf16[1,4096,64]{1,2,0:T(8,128)(2,1)S(1)}, bf16[1,4096,64]{1,2,0:T(8,128)(2,1)}, u32[]{:S(2)}) copy-start(bf16[1,4096,64]{1,2,0:T(8,128)(2,1)} %param.9) | copy-start | bytes 1572868
  4.9 6.2 %copy-start.5 = (s32[1,32]{1,0:T(1,128)S(1)}, s32[1,32]{1,0:T(1,128)}, u32[]{:S(2)}) copy-start(s32[1,32]{1,0:T(1,128)} %param.13) | copy-start | bytes 388
  5.0 6.4 %copy-start.4 = (s32[1,32,2]{1,2,0:T(2,128)S(1)}, s32[1,32,2]{1,2,0:T(2,128)}, u32[]{:S(2)}) copy-start(s32[1,32,2]{1,2,0:T(2,128)} %param.12) | copy-start | bytes 772
  6.4 15.6 %copy-start.3 = (bf16[1,64,4096]{2,1,0:T(8,128)(2,1)S(1)}, bf16[1,64,4096]{2,1,0:T(8,128)(2,1)}, u32[]{:S(2)}) copy-start(bf16[1,64,4096]{2,1,0:T(8,128)(2,1)} %param.11) | copy-start | bytes 1572868
  12.9 27.7 %all-to-all-start = ((f16[8,272,128]{2,1,0:T(8,128)(2,1)}), f16[8,272,128]{2,1,0:T(8,128)(2,1)S(1)}, u32[]{:S(2)}, u32[]{:S(2)}) async-start(f16[8,272,128]{2,1,0:T(8,128)(2,1)} %broadcast_in_dim.100), calls=%async_computation | async-start | bytes 1114112 | tf_op jit(solution)/shard_map/all_to_all | solution.py:76
  41.6 9.0 %all-to-all-start.1 = ((f32[4,64,128]{2,1,0:T(8,128)}), f32[4,64,128]{2,1,0:T(8,128)S(1)}, u32[]{:S(2)}, u32[]{:S(2)}) async-start(f32[4,64,128]{2,1,0:T(8,128)} %broadcast_in_dim.107), calls=%async_computation.1 | async-start | bytes 262144 | tf_op jit(solution)/shard_map/all_to_all | solution.py:88
  46.6 35.7 %collective-permute-start.2 = (f16[8,144,128]{2,1,0:T(8,128)(2,1)}, f16[8,144,128]{2,1,0:T(8,128)(2,1)S(1)}, u32[]{:S(2)}, u32[]{:S(2)}) collective-permute-start(f16[8,144,128]{2,1,0:T(8,128)(2,1)} %get-tuple-element.8), channel_id=1, source_target_pairs={{0,24},{8,0},{16,8},{24,16},{32,56},{40,32},{48,40},{56,48},{64,88... | collective-permute-start | bytes 884744 | tf_op jit(solution)/shard_map/ppermute | solution.py:94
  49.3 33.1 %collective-permute-start.1 = (f16[8,144,128]{2,1,0:T(8,128)(2,1)}, f16[8,144,128]{2,1,0:T(8,128)(2,1)S(1)}, u32[]{:S(2)}, u32[]{:S(2)}) collective-permute-start(f16[8,144,128]{2,1,0:T(8,128)(2,1)} %get-tuple-element.8), channel_id=1, source_target_pairs={{0,16},{8,24},{16,0},{24,8},{32,48},{40,56},{48,32},{56,40},{64,80... | collective-permute-start | bytes 884744 | tf_op jit(solution)/shard_map/ppermute | solution.py:94
  49.9 32.5 %collective-permute-start = (f16[8,144,128]{2,1,0:T(8,128)(2,1)}, f16[8,144,128]{2,1,0:T(8,128)(2,1)}, u32[]{:S(2)}, u32[]{:S(2)}) collective-permute-start(f16[8,144,128]{2,1,0:T(8,128)(2,1)} %get-tuple-element.8), channel_id=1, source_target_pairs={{0,8},{8,16},{16,24},{24,0},{32,40},{40,48},{48,56},{56,32},{64,72... | collective-permute-start | bytes 884744 | tf_op jit(solution)/shard_map/ppermute | solution.py:94

commit v2 on v0

v2 whole, which is shorter than its diff:
```python
import jax
import jax.numpy as jnp
from jax import lax
from jax.experimental import pallas as pl
from jax.experimental.pallas import tpu as pltpu
from jax.sharding import Mesh
from jax.sharding import PartitionSpec as P

E_DEV = 4
SEQ = 128
QB = 4
CAP = 2
Z = 8
Y = 4
R = 64
LANES = 128
ROWS = E_DEV * SEQ
D = 4096
F16 = jnp.float16
F32 = jnp.float32
BF16 = jnp.bfloat16
DAMP = 0.1
NT = (((1,), (1,)), ((), ()))
NN = (((1,), (0,)), ((), ()))
CHUNKS = 8
WIDTH = D // CHUNKS
MIB = 1024 * 1024

HIGH = 128
LOW = 168
NAMED = 208
PACK = 216


def dot(a, b, dims):
    return lax.dot_general(a, b, dims, preferred_element_type=F32)


def lane_iota(rows):
    return lax.broadcasted_iota(jnp.int32, (rows, LANES), 1)


def row_iota(rows):
    return lax.broadcasted_iota(jnp.int32, (rows, LANES), 0)


def swap_halves(x):
    return pltpu.roll(x, R, 1)


def exponent(m):
    return jnp.clip(jnp.floor(jnp.log2(jnp.maximum(m, 1e-30))), -96.0, 96.0)


def split(x):
    high = x.astype(BF16)
    return high, (x - high.astype(F32)).astype(BF16)


def project_kernel(
    x_hbm, g_hbm, pin_hbm, pout_hbm, me_ref, ids_ref, counts_ref, out_ref, x, g, pin, pout, acc, sem
):
    copies = []

    def fetch(src, dst):
        copy = pltpu.make_async_copy(src, dst, sem.at[len(copies)])
        copy.start()
        copies.append(copy)
        return copy

    pin_copy = fetch(pin_hbm, pin)
    x_copies, g_copies = [], []
    for c in range(CHUNKS):
        cols = slice(c * WIDTH, (c + 1) * WIDTH)
        x_copies.append(fetch(x_hbm.at[:, cols], x.at[:, cols]))
        if c == 0:
            pout_copy = fetch(pout_hbm, pout)
        g_copies.append(fetch(g_hbm.at[:, cols], g.at[:, cols]))

    own = lane_iota(1) // E_DEV == me_ref[0]
    for owner in range(Z * Y):
        for slot in range(CAP):
            block = jnp.where(slot < counts_ref[0, owner], ids_ref[slot, owner], 99)
            row = NAMED + owner % Y * CAP + slot
            out_ref[owner // Y, row : row + 1, :] = jnp.where(own, block, 0).astype(F32)

    pin_copy.wait()
    for c in range(CHUNKS):
        cols = slice(c * WIDTH, (c + 1) * WIDTH)
        x_copies[c].wait()
        xp = dot(pin[:, cols], x[:, cols], NT)
        if c == 0:
            pout_copy.wait()
        g_copies[c].wait()
        gp = dot(pout[:, cols], g[:, cols], NT)
        if c == 0:
            acc[:R] = xp
            acc[R:] = gp
        else:
            acc[:R] += xp
            acc[R:] += gp

    first = lane_iota(R) < R
    both = acc[...].astype(BF16)
    total = jnp.zeros((LANES, LANES), F32)
    powers = jnp.zeros((1, LANES), F32)
    lanes = lane_iota(1)
    examples = []
    for e in range(E_DEV):
        cols = both[:, e * SEQ : (e + 1) * SEQ]
        gram = dot(cols, cols, NT)
        total = total + gram
        example = gram[R:] * (1.0 / SEQ)
        peak = jnp.max(jnp.where(first, jnp.abs(example), 0.0), axis=(0, 1), keepdims=True)
        power = exponent(peak)
        examples.append(example * (4096.0 * jnp.exp2(-power)))
        powers = jnp.where(lanes == me_ref[0] * E_DEV + e, power, powers)
    pairs = [
        jnp.where(first, examples[0], swap_halves(examples[1])),
        jnp.where(first, examples[2], swap_halves(examples[3])),
    ]
    parts = jnp.where(first, total[:R], total[R:])
    on_diag = row_iota(R) == lane_iota(R) % R
    diag = jnp.where(on_diag, parts, 0.0)
    power_a = exponent(jnp.max(jnp.where(first, diag, 0.0), axis=(0, 1), keepdims=True))
    power_g = exponent(jnp.max(jnp.where(first, 0.0, diag), axis=(0, 1), keepdims=True))
    parts = parts * (128.0 * jnp.exp2(-jnp.where(lanes < R, power_a, power_g)))
    other = swap_halves(parts)
    mixed = jnp.where(lane_iota(R) >= row_iota(R), parts, other)
    packed = jnp.where(first[:32], mixed[:32], swap_halves(mixed[32:]))
    diag = jnp.sum(jnp.where(on_diag & first, other, 0.0), axis=0, keepdims=True)
    packed_high = jnp.round(packed * 2.0) * 0.5
    diag_high = jnp.round(diag * 2.0) * 0.5
    rows = row_iota(8)

    def tail(a, b, c, d):
        return jnp.where(
            rows == 0, a, jnp.where(rows == 1, b, jnp.where(rows == 2, c, jnp.where(rows == 3, d, 0.0)))
        )

    high_tail = tail(diag_high, power_a, power_g, powers)
    low_tail = tail((diag - diag_high) * 1024.0, 0.0, 0.0, 0.0)
    packed_low = (packed - packed_high) * 1024.0
    for z in range(Z):
        out_ref[z, 0:64, :] = pairs[0]
        out_ref[z, 64:128, :] = pairs[1]
        out_ref[z, HIGH : HIGH + 32, :] = packed_high
        out_ref[z, HIGH + 32 : LOW, :] = high_tail
        out_ref[z, LOW : LOW + 32, :] = packed_low
        out_ref[z, LOW + 32 : NAMED, :] = low_tail


def project(x, g, pin, pout, me, ids, counts):
    hbm = pl.BlockSpec(memory_space=pl.ANY)
    smem = pl.BlockSpec(memory_space=pltpu.SMEM)
    return pl.pallas_call(
        project_kernel,
        out_shape=jax.ShapeDtypeStruct((Z, PACK, LANES), F32),
        in_specs=[hbm, hbm, hbm, hbm, smem, smem, smem],
        out_specs=pl.BlockSpec(memory_space=pltpu.VMEM),
        scratch_shapes=[
            pltpu.VMEM((ROWS, D), BF16),
            pltpu.VMEM((ROWS, D), BF16),
            pltpu.VMEM((R, D), BF16),
            pltpu.VMEM((R, D), BF16),
            pltpu.VMEM((LANES, ROWS), F32),
            pltpu.SemaphoreType.DMA((2 + 2 * CHUNKS,)),
        ],
        compiler_params=pltpu.CompilerParams(vmem_limit_bytes=60 * MIB),
        name="project",
    )(x, g, pin, pout, me, ids, counts)


def invert_pair(m):
    lanes = lane_iota(R)
    rows = row_iota(R)
    half = jnp.where(lanes < R, 0, R)
    local = lane_iota(1) % R
    for k in range(0, R, 2):
        c0 = jnp.take_along_axis(m, half + k, axis=1)
        c1 = jnp.take_along_axis(m, half + (k + 1), axis=1)
        r0 = m[k : k + 1]
        r1 = m[k + 1 : k + 2]
        p00 = c0[k : k + 1]
        p10 = c0[k + 1 : k + 2]
        p01 = c1[k : k + 1]
        p11 = c1[k + 1 : k + 2]
        inv = 1.0 / (p00 * p11 - p01 * p10)
        is0 = local == k
        is1 = local == k + 1
        r0 = jnp.where(is0, 1.0, jnp.where(is1, 0.0, r0))
        r1 = jnp.where(is1, 1.0, jnp.where(is0, 0.0, r1))
        q0 = (p11 * r0 - p01 * r1) * inv
        q1 = (p00 * r1 - p10 * r0) * inv
        kept = jnp.where(is0 | is1, 0.0, m)
        m = kept - c0 * q0 - c1 * q1
        m = jnp.where(rows == k, q0, jnp.where(rows == k + 1, q1, m))
    return m


def block_diagonal(a):
    wide = jnp.concatenate([a, a], axis=1)
    tall = jnp.concatenate([wide, wide, wide, wide], axis=0)
    r = lax.broadcasted_iota(jnp.int32, (4 * R, 4 * R), 0) // R
    c = lax.broadcasted_iota(jnp.int32, (4 * R, 4 * R), 1) // R
    return jnp.where(r == c, tall, 0.0)


def score_kernel(tokens, scale, parts_ref, t_ref, info_ref, y_ref, *refs):
    queries, out_ref, lh, ll, u, tp = refs[:Y], *refs[Y:]
    total = jnp.sum(parts_ref[...], axis=0)
    first = lane_iota(R) < R
    row, col = row_iota(R), lane_iota(R) % R
    packed = total[:32]
    moved = swap_halves(packed)
    mixed = jnp.concatenate(
        [jnp.where(first[:32], packed, moved), jnp.where(first[:32], moved, packed)], axis=0
    )
    turned = jnp.concatenate([mixed, mixed], axis=0).T[:R]
    diag_g = total[32:33]
    diag_g = jnp.where(first[:1], diag_g, swap_halves(diag_g))
    factor_a = jnp.where(col >= row, mixed, turned)
    factor_g = jnp.where(col < row, mixed, jnp.where(col > row, turned, diag_g))
    m = jnp.where(first, factor_a, factor_g) * (1.0 / tokens)
    on_diag = row == col
    diag = jnp.sum(jnp.where(on_diag, m, 0.0), axis=0, keepdims=True)
    trace_a = jnp.sum(jnp.where(first[:1], diag, 0.0), axis=1, keepdims=True)
    trace_g = jnp.sum(jnp.where(first[:1], 0.0, diag), axis=1, keepdims=True)
    damp = (DAMP / R) * jnp.where(first[:1], trace_a, trace_g) + 1e-06
    m = invert_pair(jnp.where(on_diag, m + damp, m))
    other = swap_halves(m)
    ia = block_diagonal(jnp.where(first, m, other))
    ig = jnp.where(first, other, m)[:, :R]

    g0 = ig.astype(BF16)
    g1, g2 = split(ig - g0.astype(F32))
    left = jnp.concatenate([g0, g1, g2], axis=0)
    for z in range(Z):
        block = t_ref[z]
        th, tl = split(jnp.concatenate([block[:R], block[R:]], axis=1))
        p = dot(left, th, NN)
        q = dot(left[: 2 * R], tl, NN)
        high, low = split(p[:R] + ((p[R : 2 * R] + q[:R]) + (p[2 * R :] + q[R:])))
        lh[z * R : (z + 1) * R, :] = high
        ll[z * R : (z + 1) * R, :] = low
    ah, al = split(ia)
    for c in range(2):
        rows = slice(c * 256, (c + 1) * 256)
        high = lh[rows, :]
        p = dot(high, ah, NN) + (dot(ll[rows, :], ah, NN) + dot(high, al, NN))
        for s in range(4):
            for t in range(2):
                pair = (c * 4 + s) * 2 + t
                u[pair * R : (pair + 1) * R, :] = p[s * R : (s + 1) * R, t * 128 : (t + 1) * 128]
    low_half = first[:16]
    for i in range(0, R, 2):
        w0 = u[pl.ds(i, 16, stride=R), :]
        w1 = u[pl.ds(i + 1, 16, stride=R), :]
        cols = slice(i * R, (i + 2) * R)
        tp[0:16, cols] = jnp.where(low_half, w0, swap_halves(w1)).astype(BF16)
        tp[16:32, cols] = jnp.where(low_half, swap_halves(w0), w1).astype(BF16)

    my_y = y_ref[0]
    s = jnp.concatenate([dot(queries[k][...], tp[...], NT) for k in range(Y)], axis=0)
    take = row_iota(32)
    place = take % 16 // 2 * (Y * E_DEV) + my_y * E_DEV + take % 2 * 2 + take // 16
    onehot = jnp.where(place == lane_iota(32), 1.0, 0.0).astype(BF16)
    s0 = s.astype(BF16)
    s1, s2 = split(s - s0.astype(F32))
    s = dot(s0, onehot, NN) + (dot(s1, onehot, NN) + dot(s2, onehot, NN))
    column = jnp.exp2(info_ref[8:9, :]) * scale
    blocks = (row // QB).astype(F32)
    for k in range(Y):
        owner = (my_y + Y - k) % Y
        id0, id1 = info_ref[0:1, :], info_ref[1:2, :]
        for y in range(1, Y):
            id0 = jnp.where(owner == y, info_ref[2 * y : 2 * y + 1, :], id0)
            id1 = jnp.where(owner == y, info_ref[2 * y + 1 : 2 * y + 2, :], id1)
        live = (blocks == id0) | (blocks == id1)
        out_ref[owner] = jnp.where(live, s[k * R : (k + 1) * R] * column, 0.0)


def score(parts, train, info, y, queries, tokens, scale):
    vmem = pl.BlockSpec(memory_space=pltpu.VMEM)
    smem = pl.BlockSpec(memory_space=pltpu.SMEM)
    return pl.pallas_call(
        lambda *refs: score_kernel(float(tokens), scale, *refs),
        out_shape=jax.ShapeDtypeStruct((Y, R, LANES), F32),
        in_specs=[vmem, vmem, vmem, smem] + [vmem] * Y,
        out_specs=vmem,
        scratch_shapes=[
            pltpu.VMEM((Z * R, 256), BF16),
            pltpu.VMEM((Z * R, 256), BF16),
            pltpu.VMEM((2 * Z * R, LANES), F32),
            pltpu.VMEM((Z * E_DEV, D), BF16),
        ],
        compiler_params=pltpu.CompilerParams(vmem_limit_bytes=32 * MIB),
        name="score",
    )(parts, train, info, y, *queries)


def body(x_act, g_out, proj_in, proj_out, queries, cand_ids, cand_counts):
    n_layers = lax.axis_size("block")
    my_y = lax.axis_index("y").astype(jnp.int32)
    me = lax.axis_index("z").astype(jnp.int32) * Y + my_y
    query = [queries[0]]
    for k in range(1, Y):
        query.append(lax.ppermute(queries[0], "y", [(y, (y + k) % Y) for y in range(Y)]))
    packet = project(
        x_act[0],
        g_out[0],
        proj_in[0].T,
        proj_out[0].T,
        jnp.reshape(me, (1,)),
        cand_ids[0].T,
        cand_counts,
    )
    got = lax.all_to_all(packet.astype(F16), "z", 0, 0, tiled=True)

    r = jnp.arange(40)[:, None]
    lane = jnp.arange(LANES)[None, :]
    upper = (lane % R >= r + R // 2 * (lane // R)) & (r < 32)
    power = jnp.where(
        upper[None],
        got[:, HIGH + 33 : HIGH + 34].astype(F32),
        got[:, HIGH + 34 : HIGH + 35].astype(F32),
    )
    both = got[:, HIGH:LOW].astype(F32) + got[:, LOW:NAMED].astype(F32) * (1.0 / 1024.0)
    sums = jnp.sum(both * (jnp.exp2(power) * (1.0 / 128.0)), axis=0)
    spread = jnp.broadcast_to(sums[None], (Y,) + sums.shape)
    spread, got = lax.optimization_barrier((spread, got))
    parts = lax.all_to_all(spread, "y", 0, 0, tiled=True)

    train = got[:, :128].astype(F32)
    info = jnp.concatenate(
        [
            jnp.sum(got[:, NAMED:].astype(F32), axis=0),
            jnp.sum(got[:, HIGH + 35 : HIGH + 43].astype(F32), axis=0),
        ],
        axis=0,
    )
    scale = 1.0 / float(R * R * n_layers) ** 0.5 / 4096.0
    tokens = ROWS * Z * Y
    scores = score(parts, train, info, jnp.reshape(my_y, (1,)), query, tokens, scale)
    scores = scores.reshape(Y * n_layers, R // n_layers, LANES)
    return jnp.sum(lax.all_to_all(scores, ("y", "block"), 0, 0, tiled=True), axis=0)


def solution(mesh):
    split_mesh = Mesh(mesh.devices.reshape(Z, Y, -1), ("z", "y", "block"))
    shard = ("z", "y")
    return jax.shard_map(
        body,
        mesh=split_mesh,
        in_specs=(
            P("block", shard, None),
            P("block", shard, None),
            P("block", None, None),
            P("block", None, None),
            P("block", shard, None),
            P(shard, None, None),
            P(shard, None),
        ),
        out_specs=P(("z", "y", "block"), None),
        check_vma=False,
    )
```

time: 292 us -> 66.9 us (0.23)
  blocking collectives: 144 us -> 14.4 us
  waiting for transfers between devices: 82.6 us -> 18.1 us
  other arithmetic: 26.1 us -> 2.85 us
  between operations: 15.6 us -> 0.06 us
  Pallas kernels: 0 us -> 12.2 us
  starting transfers between devices: 7.64 us -> 18.3 us
  matrix products: 7.64 us -> 0 us
  local copies, waits for them, and re-layouts: 6.72 us -> 0.63 us
    psum x1 -> x0, blocking collectives: 119 us -> none  [body(): factor_a, factor_g = lax.psum((part_a, part_g), 'dp')]
    all_gather x1 -> x0, waiting for transfers between devices: 68.2 us -> none  [body(): lax.all_gather(precond, 'dp', axis=0, tiled=True)]
    unnamed x1 -> x0, blocking collectives: 25.1 us -> none
    another operation x10 -> x0, other arithmetic: 24.1 us -> none  [the longest x6 13 us: kron_inverse(): lower_factor = jnp.linalg.cholesky(factor + damping * identity)]
    all_to_all x0 -> x1, blocking collectives: none -> 14.4 us  [body(): lax.all_to_all(scores, ('y', 'block'), 0, 0, tiled=True)]
    pallas_call x0 -> x2, Pallas kernels: none -> 12.2 us  [the longest x1 6.82 us: project(): pl.pallas_call(project_kernel, out_shape=jax.ShapeDtypeStruct((Z, PACK, L...]
    dot_general x8 -> x0, matrix products: 6.81 us -> none  [the longest x1 3.73 us: body(): jnp.dot(grad_rows, proj_out[0], preferred_element_type=jnp.float32)]
    all_to_all x2, starting transfers between devices: 7.64 us -> 13.2 us  [the longest x1 9.02 us: body(): got = lax.all_to_all(packet.astype(F16), 'z', 0, 0, tiled=True)]
  transfers between devices with their start and end apart: 3 -> 5, of which waited for: 3 -> 3; matrix products, arithmetic and copies ran while one was open for 1% -> 1% of each run, Pallas kernels for 0% -> 0%
where the time goes in v2:
time: 66.9 us; the launch traced here: 66.5 us
  starting transfers between devices  18.3 us (27%)
  waiting for transfers between devices  18.1 us (27%)
  blocking collectives  14.4 us (22%)
  Pallas kernels  12.2 us (18%)
  other arithmetic  2.85 us (4%)
    all_to_all x1, blocking collectives, body(): lax.all_to_all(scores, ('y', 'block'), 0, 0, tiled=True)  14.4 us
    all_to_all x1, waiting for transfers between devices, body(): got = lax.all_to_all(packet.astype(F16), 'z', 0, 0, tiled=True)  10.7 us
    all_to_all x1, starting transfers between devices, body(): got = lax.all_to_all(packet.astype(F16), 'z', 0, 0, tiled=True)  9.02 us
    pallas_call x1, Pallas kernels, project(): pl.pallas_call(project_kernel, out_shape=jax.ShapeDtypeStruct((Z, PACK, L...  6.82 us
    ppermute x3, waiting for transfers between devices, body(): lax.ppermute(queries[0], 'y', [(y, (y + k) % Y) for y in range(Y)])  5.45 us
    pallas_call x1, Pallas kernels, score(): pl.pallas_call(lambda *refs: score_kernel(float(tokens), scale, *refs), o...  5.38 us
    ppermute x3, starting transfers between devices, body(): lax.ppermute(queries[0], 'y', [(y, (y + k) % Y) for y in range(Y)])  5.06 us
    all_to_all x1, starting transfers between devices, body(): parts = lax.all_to_all(spread, 'y', 0, 0, tiled=True)  4.19 us
  transfers between devices with their start and end apart: 5, of which 3 were waited for; matrix products, arithmetic and copies ran while one was open for 1% of the time, Pallas kernels for 0%

profile of v2, /device:TPU:1, one launch (start us, length us, event | category | flops | bytes accessed | tf_op | source)
XLA Modules:
  0.0 66.5 jit_solution(15684583729182573237)
XLA Ops:
  0.0 0.0 copy-start
  0.0 6.8 %project.1 = f32[8,216,128]{2,1,0:T(8,128)} custom-call(bf16[512,4096]{1,0:T(8,128)(2,1)} %bitcast.22, bf16[512,4096]{1,0:T(8,128)(2,1)} %bitcast.23, bf16[64,4096]{1,0:T(8,128)(2,1)} %bitcast.24, bf16[64,4096]{1,0:T(8,128)(2,1)} %bitcast.25, s32[1]{0:T(128)} %bitcast.6.me_ref, s32[2,32]{1,0:T(2,128)} %bitcast.28, s32[1,32]{1,0:T(1,128)} %counts_ref.1), custom_call_target="tpu_custom_call" | custom-call | tf_op jit(solution)/shard_map/project/pallas_call | solution.py:156
  6.8 2.0 %convert_element_type.20 = f16[8,216,128]{2,1,0:T(8,128)(2,1)} convert(f32[8,216,128]{2,1,0:T(8,128)} %project.1) | non-fusion elementwise | flops 221184 | bytes 1327104 | tf_op jit(solution)/shard_map/convert_element_type | solution.py:318
  8.8 9.0 %all-to-all-start = ((f16[8,216,128]{2,1,0:T(8,128)(2,1)}), f16[8,216,128]{2,1,0:T(8,128)(2,1)S(1)}, u32[]{:S(2)}, u32[]{:S(2)}) async-start(f16[8,216,128]{2,1,0:T(8,128)(2,1)} %convert_element_type.20), calls=%async_computation | async-start | bytes 884736 | tf_op jit(solution)/shard_map/all_to_all | solution.py:318
  17.9 0.0 copy-done
  17.9 1.4 %collective-permute-start = (bf16[64,4096]{1,0:T(8,128)(2,1)S(1)}, bf16[64,4096]{1,0:T(8,128)(2,1)S(1)}, u32[]{:S(2)}, u32[]{:S(2)}) collective-permute-start(bf16[64,4096]{1,0:T(8,128)(2,1)S(1)} %bitcast.18), channel_id=1, source_target_pairs={{0,8},{8,16},{16,24},{24,0},{1,9},{9,17},{17,25},{25,1},{2,10},{10... | collective-permute-start | bytes 1572872 | tf_op jit(solution)/shard_map/ppermute | solution.py:308
  19.2 2.6 %collective-permute-start.1 = (bf16[64,4096]{1,0:T(8,128)(2,1)S(1)}, bf16[64,4096]{1,0:T(8,128)(2,1)S(1)}, u32[]{:S(2)}, u32[]{:S(2)}) collective-permute-start(bf16[64,4096]{1,0:T(8,128)(2,1)S(1)} %bitcast.19), channel_id=1, source_target_pairs={{0,16},{8,24},{16,0},{24,8},{1,17},{9,25},{17,1},{25,9},{2,18},{10... | collective-permute-start | bytes 1572872 | tf_op jit(solution)/shard_map/ppermute | solution.py:308
  21.9 1.1 %collective-permute-start.2 = (bf16[64,4096]{1,0:T(8,128)(2,1)S(1)}, bf16[64,4096]{1,0:T(8,128)(2,1)S(1)}, u32[]{:S(2)}, u32[]{:S(2)}) collective-permute-start(bf16[64,4096]{1,0:T(8,128)(2,1)S(1)} %bitcast.20), channel_id=1, source_target_pairs={{0,24},{8,0},{16,8},{24,16},{1,25},{9,1},{17,9},{25,17},{2,26},{10... | collective-permute-start | bytes 1572872 | tf_op jit(solution)/shard_map/ppermute | solution.py:308
  22.9 0.1 fusion
  23.0 10.7 %all-to-all-done = f16[8,216,128]{2,1,0:T(8,128)(2,1)S(1)} async-done(((f16[8,216,128]{2,1,0:T(8,128)(2,1)}), f16[8,216,128]{2,1,0:T(8,128)(2,1)S(1)}, u32[]{:S(2)}, u32[]{:S(2)}) %all-to-all-start) | async-done | bytes 442400 | tf_op jit(solution)/shard_map/all_to_all | solution.py:318
  33.7 0.1 multiply_reduce_fusion
  33.8 0.6 broadcast_in_dim.50
  34.4 4.2 %all-to-all-start.1 = ((f32[4,40,128]{2,1,0:T(8,128)}), f32[4,40,128]{2,1,0:T(8,128)S(1)}, u32[]{:S(2)}, u32[]{:S(2)}) async-start(f32[4,40,128]{2,1,0:T(8,128)} %broadcast_in_dim.50), calls=%async_computation.1 | async-start | bytes 163840 | tf_op jit(solution)/shard_map/all_to_all | solution.py:332
  38.6 0.0 collective-permute-done.refs_5_
  38.7 5.4 %collective-permute-done.1.refs_6_ = bf16[64,4096]{1,0:T(8,128)(2,1)S(1)} collective-permute-done((bf16[64,4096]{1,0:T(8,128)(2,1)S(1)}, bf16[64,4096]{1,0:T(8,128)(2,1)S(1)}, u32[]{:S(2)}, u32[]{:S(2)}) %collective-permute-start.1) | collective-permute-done | bytes 524320 | tf_op jit(solution)/shard_map/ppermute | solution.py:308
  44.1 0.0 collective-permute-done.2.refs_7_
  44.1 2.0 %all-to-all-done.1.refs_0_ = f32[4,40,128]{2,1,0:T(8,128)S(1)} async-done(((f32[4,40,128]{2,1,0:T(8,128)}), f32[4,40,128]{2,1,0:T(8,128)S(1)}, u32[]{:S(2)}, u32[]{:S(2)}) %all-to-all-start.1) | async-done | bytes 81952 | tf_op jit(solution)/shard_map/all_to_all | solution.py:332
  46.1 5.4 %score.1 = f32[4,64,128]{2,1,0:T(8,128)S(1)} custom-call(f32[4,40,128]{2,1,0:T(8,128)S(1)} %all-to-all-done.1.refs_0_, f32[8,128,128]{2,1,0:T(8,128)S(1)} %slice_convert_fusion.refs_1_, f32[16,128]{1,0:T(8,128)S(1)} %pad_maximum_fusion.refs_2_, s32[1]{0:T(128)} %bitcast.11.refs_3_, bf16[64,4096]{1,0:T(8,128)(2,1)S(1)} %bitcast.21, ...), custom_call_target="tpu_custom_call" | custom-call | tf_op jit(solution)/shard_map/score/pallas_call | solution.py:286
  51.5 14.4 %all_to_all.15 = f32[32,8,128]{2,1,0:T(8,128)S(1)} all-to-all(f32[32,8,128]{2,1,0:T(8,128)S(1)} %bitcast.17), channel_id=1, replica_groups=mesh['z'=8,'y'=4,'block'=8] {'y','block'}, dimensions={0} | all-to-all | bytes 262144 | tf_op jit(solution)/shard_map/all_to_all | solution.py:346
  65.9 0.6 reduce_sum.39
  (6 shorter events, 0.1 us)
Async XLA Ops:
  0.0 17.9 %copy-start = (bf16[1,64,4096]{2,1,0:T(8,128)(2,1)S(1)}, bf16[1,64,4096]{2,1,0:T(8,128)(2,1)}, u32[]{:S(2)}) copy-start(bf16[1,64,4096]{2,1,0:T(8,128)(2,1)} %param.11) | copy-start | bytes 1572868
  8.8 24.8 %all-to-all-start = ((f16[8,216,128]{2,1,0:T(8,128)(2,1)}), f16[8,216,128]{2,1,0:T(8,128)(2,1)S(1)}, u32[]{:S(2)}, u32[]{:S(2)}) async-start(f16[8,216,128]{2,1,0:T(8,128)(2,1)} %convert_element_type.20), calls=%async_computation | async-start | bytes 884736 | tf_op jit(solution)/shard_map/all_to_all | solution.py:318
  17.9 20.8 %collective-permute-start = (bf16[64,4096]{1,0:T(8,128)(2,1)S(1)}, bf16[64,4096]{1,0:T(8,128)(2,1)S(1)}, u32[]{:S(2)}, u32[]{:S(2)}) collective-permute-start(bf16[64,4096]{1,0:T(8,128)(2,1)S(1)} %bitcast.18), channel_id=1, source_target_pairs={{0,8},{8,16},{16,24},{24,0},{1,9},{9,17},{17,25},{25,1},{2,10},{10... | collective-permute-start | bytes 1572872 | tf_op jit(solution)/shard_map/ppermute | solution.py:308
  19.2 24.9 %collective-permute-start.1 = (bf16[64,4096]{1,0:T(8,128)(2,1)S(1)}, bf16[64,4096]{1,0:T(8,128)(2,1)S(1)}, u32[]{:S(2)}, u32[]{:S(2)}) collective-permute-start(bf16[64,4096]{1,0:T(8,128)(2,1)S(1)} %bitcast.19), channel_id=1, source_target_pairs={{0,16},{8,24},{16,0},{24,8},{1,17},{9,25},{17,1},{25,9},{2,18},{10... | collective-permute-start | bytes 1572872 | tf_op jit(solution)/shard_map/ppermute | solution.py:308
  21.9 22.2 %collective-permute-start.2 = (bf16[64,4096]{1,0:T(8,128)(2,1)S(1)}, bf16[64,4096]{1,0:T(8,128)(2,1)S(1)}, u32[]{:S(2)}, u32[]{:S(2)}) collective-permute-start(bf16[64,4096]{1,0:T(8,128)(2,1)S(1)} %bitcast.20), channel_id=1, source_target_pairs={{0,24},{8,0},{16,8},{24,16},{1,25},{9,1},{17,9},{25,17},{2,26},{10... | collective-permute-start | bytes 1572872 | tf_op jit(solution)/shard_map/ppermute | solution.py:308
  34.4 11.7 %all-to-all-start.1 = ((f32[4,40,128]{2,1,0:T(8,128)}), f32[4,40,128]{2,1,0:T(8,128)S(1)}, u32[]{:S(2)}, u32[]{:S(2)}) async-start(f32[4,40,128]{2,1,0:T(8,128)} %broadcast_in_dim.50), calls=%async_computation.1 | async-start | bytes 163840 | tf_op jit(solution)/shard_map/all_to_all | solution.py:332

commit v3 on v2

--- a/solution.py
+++ b/solution.py
@@ -22,14 +22,15 @@
 DAMP = 0.1
 NT = (((1,), (1,)), ((), ()))
 NN = (((1,), (0,)), ((), ()))
+TN = (((0,), (0,)), ((), ()))
 CHUNKS = 8
 WIDTH = D // CHUNKS
 MIB = 1024 * 1024
 
 HIGH = 128
+NOTES = 160
 LOW = 168
-NAMED = 208
-PACK = 216
+PACK = 200
 
 
 def dot(a, b, dims):
@@ -77,12 +78,12 @@
             pout_copy = fetch(pout_hbm, pout)
         g_copies.append(fetch(g_hbm.at[:, cols], g.at[:, cols]))
 
-    own = lane_iota(1) // E_DEV == me_ref[0]
+    lanes = lane_iota(1)
+    named = jnp.zeros((1, LANES), jnp.int32)
     for owner in range(Z * Y):
         for slot in range(CAP):
             block = jnp.where(slot < counts_ref[0, owner], ids_ref[slot, owner], 99)
-            row = NAMED + owner % Y * CAP + slot
-            out_ref[owner // Y, row : row + 1, :] = jnp.where(own, block, 0).astype(F32)
+            named = jnp.where(lanes == owner * CAP + slot, block, named)
 
     pin_copy.wait()
     for c in range(CHUNKS):
@@ -102,52 +103,44 @@
 
     first = lane_iota(R) < R
     both = acc[...].astype(BF16)
+    on_diag = row_iota(R) == lane_iota(R) % R
     total = jnp.zeros((LANES, LANES), F32)
-    powers = jnp.zeros((1, LANES), F32)
-    lanes = lane_iota(1)
-    examples = []
+    examples, peaks = [], []
     for e in range(E_DEV):
         cols = both[:, e * SEQ : (e + 1) * SEQ]
         gram = dot(cols, cols, NT)
         total = total + gram
-        example = gram[R:] * (1.0 / SEQ)
-        peak = jnp.max(jnp.where(first, jnp.abs(example), 0.0), axis=(0, 1), keepdims=True)
-        power = exponent(peak)
-        examples.append(example * (4096.0 * jnp.exp2(-power)))
-        powers = jnp.where(lanes == me_ref[0] * E_DEV + e, power, powers)
-    pairs = [
-        jnp.where(first, examples[0], swap_halves(examples[1])),
-        jnp.where(first, examples[2], swap_halves(examples[3])),
-    ]
+        example = jnp.where(first, gram[R:], 0.0) * (1.0 / SEQ)
+        examples.append(example)
+        peaks.append(jnp.max(jnp.abs(example), axis=0, keepdims=True))
     parts = jnp.where(first, total[:R], total[R:])
-    on_diag = row_iota(R) == lane_iota(R) % R
-    diag = jnp.where(on_diag, parts, 0.0)
-    power_a = exponent(jnp.max(jnp.where(first, diag, 0.0), axis=(0, 1), keepdims=True))
-    power_g = exponent(jnp.max(jnp.where(first, 0.0, diag), axis=(0, 1), keepdims=True))
-    parts = parts * (128.0 * jnp.exp2(-jnp.where(lanes < R, power_a, power_g)))
+    diag = jnp.max(jnp.where(on_diag, parts, 0.0), axis=0, keepdims=True)
+    peaks.append(jnp.where(first[:1], diag, 0.0))
+    peaks.append(jnp.where(first[:1], 0.0, diag))
+    peaks.append(jnp.zeros((2, LANES), F32))
+    power = exponent(jnp.max(jnp.concatenate(peaks, axis=0), axis=1, keepdims=True))
+    grow = 4096.0 * jnp.exp2(-power)
+    powers = jnp.zeros((1, LANES), F32)
+    for e in range(E_DEV):
+        examples[e] = examples[e] * grow[e : e + 1]
+        powers = jnp.where(lanes == me_ref[0] * E_DEV + e, power[e : e + 1], powers)
+    out_ref[0:64, :] = jnp.where(first, examples[0], swap_halves(examples[1]))
+    out_ref[64:128, :] = jnp.where(first, examples[2], swap_halves(examples[3]))
+    parts = parts * (jnp.where(lanes < R, grow[4:5], grow[5:6]) * (1.0 / 32.0))
     other = swap_halves(parts)
     mixed = jnp.where(lane_iota(R) >= row_iota(R), parts, other)
     packed = jnp.where(first[:32], mixed[:32], swap_halves(mixed[32:]))
-    diag = jnp.sum(jnp.where(on_diag & first, other, 0.0), axis=0, keepdims=True)
-    packed_high = jnp.round(packed * 2.0) * 0.5
+    diag = jnp.sum(jnp.where(on_diag, jnp.where(first, other, parts), 0.0), axis=0, keepdims=True)
+    high = jnp.round(packed * 2.0) * 0.5
     diag_high = jnp.round(diag * 2.0) * 0.5
+    diag = jnp.where(first[:1], diag_high, (diag - diag_high) * 1024.0)
     rows = row_iota(8)
-
-    def tail(a, b, c, d):
-        return jnp.where(
-            rows == 0, a, jnp.where(rows == 1, b, jnp.where(rows == 2, c, jnp.where(rows == 3, d, 0.0)))
-        )
-
-    high_tail = tail(diag_high, power_a, power_g, powers)
-    low_tail = tail((diag - diag_high) * 1024.0, 0.0, 0.0, 0.0)
-    packed_low = (packed - packed_high) * 1024.0
-    for z in range(Z):
-        out_ref[z, 0:64, :] = pairs[0]
-        out_ref[z, 64:128, :] = pairs[1]
-        out_ref[z, HIGH : HIGH + 32, :] = packed_high
-        out_ref[z, HIGH + 32 : LOW, :] = high_tail
-        out_ref[z, LOW : LOW + 32, :] = packed_low
-        out_ref[z, LOW + 32 : NAMED, :] = low_tail
+    notes = jnp.zeros((8, LANES), F32)
+    for i, line in enumerate([diag, power[4:5], power[5:6], powers, named.astype(F32)]):
+        notes = jnp.where(rows == i, line, notes)
+    out_ref[HIGH:NOTES, :] = high
+    out_ref[NOTES:LOW, :] = notes
+    out_ref[LOW:PACK, :] = (packed - high) * 1024.0
 
 
 def project(x, g, pin, pout, me, ids, counts):
@@ -155,7 +148,7 @@
     smem = pl.BlockSpec(memory_space=pltpu.SMEM)
     return pl.pallas_call(
         project_kernel,
-        out_shape=jax.ShapeDtypeStruct((Z, PACK, LANES), F32),
+        out_shape=jax.ShapeDtypeStruct((PACK, LANES), F32),
         in_specs=[hbm, hbm, hbm, hbm, smem, smem, smem],
         out_specs=pl.BlockSpec(memory_space=pltpu.VMEM),
         scratch_shapes=[
@@ -206,9 +199,8 @@
     return jnp.where(r == c, tall, 0.0)
 
 
-def score_kernel(tokens, scale, parts_ref, t_ref, info_ref, y_ref, *refs):
-    queries, out_ref, lh, ll, u, tp = refs[:Y], *refs[Y:]
-    total = jnp.sum(parts_ref[...], axis=0)
+def solve_kernel(tokens, p0, p1, p2, p3, t_ref, tp, lh, ll, u):
+    total = (p0[...] + p2[...]) + (p1[...] + p3[...])
     first = lane_iota(R) < R
     row, col = row_iota(R), lane_iota(R) % R
     packed = total[:32]
@@ -218,7 +210,8 @@
     )
     turned = jnp.concatenate([mixed, mixed], axis=0).T[:R]
     diag_g = total[32:33]
-    diag_g = jnp.where(first[:1], diag_g, swap_halves(diag_g))
+    moved = swap_halves(diag_g)
+    diag_g = jnp.where(first[:1], diag_g, moved) + jnp.where(first[:1], moved, diag_g) * (1.0 / 1024.0)
     factor_a = jnp.where(col >= row, mixed, turned)
     factor_g = jnp.where(col < row, mixed, jnp.where(col > row, turned, diag_g))
     m = jnp.where(first, factor_a, factor_g) * (1.0 / tokens)
@@ -236,8 +229,7 @@
     g1, g2 = split(ig - g0.astype(F32))
     left = jnp.concatenate([g0, g1, g2], axis=0)
     for z in range(Z):
-        block = t_ref[z]
-        th, tl = split(jnp.concatenate([block[:R], block[R:]], axis=1))
+        th, tl = split(jnp.concatenate([t_ref[z, :R, :], t_ref[z, R : 2 * R, :]], axis=1))
         p = dot(left, th, NN)
         q = dot(left[: 2 * R], tl, NN)
         high, low = split(p[:R] + ((p[R : 2 * R] + q[:R]) + (p[2 * R :] + q[R:])))
@@ -260,52 +252,81 @@
         tp[0:16, cols] = jnp.where(low_half, w0, swap_halves(w1)).astype(BF16)
         tp[16:32, cols] = jnp.where(low_half, swap_halves(w0), w1).astype(BF16)
 
-    my_y = y_ref[0]
-    s = jnp.concatenate([dot(queries[k][...], tp[...], NT) for k in range(Y)], axis=0)
+
+def score_kernel(scale, tp, got_ref, at_ref, *refs):
+    queries, out_ref, names = refs[: Y + 1], *refs[Y + 1 :]
+    my_z, my_y = at_ref[0], at_ref[1]
+    s = jnp.concatenate([dot(queries[k][...], tp[...], NT) for k in range(Y + 1)], axis=0)
     take = row_iota(32)
     place = take % 16 // 2 * (Y * E_DEV) + my_y * E_DEV + take % 2 * 2 + take // 16
     onehot = jnp.where(place == lane_iota(32), 1.0, 0.0).astype(BF16)
     s0 = s.astype(BF16)
     s1, s2 = split(s - s0.astype(F32))
     s = dot(s0, onehot, NN) + (dot(s1, onehot, NN) + dot(s2, onehot, NN))
-    column = jnp.exp2(info_ref[8:9, :]) * scale
-    blocks = (row // QB).astype(F32)
+    lanes = lane_iota(2 * Z)
+    mine = (lanes // (Y * E_DEV) == row_iota(2 * Z)) & (lanes // E_DEV % Y == my_y)
+    power = jnp.zeros((1, LANES), F32)
+    listed = []
+    for z in range(Z):
+        power = power + got_ref[z, NOTES + 3 : NOTES + 4, :]
+        listed.append(got_ref[z, NOTES + 4 : NOTES + 5, :])
+    listed = jnp.concatenate(listed + [jnp.zeros((Z, LANES), F32)], axis=0).astype(BF16)
+    names[...] = dot(listed, jnp.where(mine, 1.0, 0.0).astype(BF16), TN)
+    named = names[pl.ds(pl.multiple_of(my_z * (Y * CAP), Y * CAP), Y * CAP), :]
+    column = jnp.exp2(power) * scale
+    blocks = (row_iota(R) // QB).astype(F32)
     for k in range(Y):
         owner = (my_y + Y - k) % Y
-        id0, id1 = info_ref[0:1, :], info_ref[1:2, :]
+        id0, id1 = named[0:1], named[1:2]
         for y in range(1, Y):
-            id0 = jnp.where(owner == y, info_ref[2 * y : 2 * y + 1, :], id0)
-            id1 = jnp.where(owner == y, info_ref[2 * y + 1 : 2 * y + 2, :], id1)
+            id0 = jnp.where(owner == y, named[2 * y : 2 * y + 1], id0)
+            id1 = jnp.where(owner == y, named[2 * y + 1 : 2 * y + 2], id1)
         live = (blocks == id0) | (blocks == id1)
         out_ref[owner] = jnp.where(live, s[k * R : (k + 1) * R] * column, 0.0)
 
 
-def score(parts, train, info, y, queries, tokens, scale):
+def solve(parts, train, tokens):
     vmem = pl.BlockSpec(memory_space=pltpu.VMEM)
-    smem = pl.BlockSpec(memory_space=pltpu.SMEM)
     return pl.pallas_call(
-        lambda *refs: score_kernel(float(tokens), scale, *refs),
-        out_shape=jax.ShapeDtypeStruct((Y, R, LANES), F32),
-        in_specs=[vmem, vmem, vmem, smem] + [vmem] * Y,
+        lambda *refs: solve_kernel(float(tokens), *refs),
+        out_shape=jax.ShapeDtypeStruct((Z * E_DEV, D), BF16),
+        in_specs=[vmem] * (Y + 1),
         out_specs=vmem,
         scratch_shapes=[
             pltpu.VMEM((Z * R, 256), BF16),
             pltpu.VMEM((Z * R, 256), BF16),
             pltpu.VMEM((2 * Z * R, LANES), F32),
-            pltpu.VMEM((Z * E_DEV, D), BF16),
         ],
         compiler_params=pltpu.CompilerParams(vmem_limit_bytes=32 * MIB),
+        cost_estimate=pl.CostEstimate(flops=4 * 10**9, bytes_accessed=2 * MIB, transcendentals=0),
+        name="solve",
+    )(*parts, train)
+
+
+def score(tp, got, at, queries, scale):
+    vmem = pl.BlockSpec(memory_space=pltpu.VMEM)
+    smem = pl.BlockSpec(memory_space=pltpu.SMEM)
+    return pl.pallas_call(
+        lambda *refs: score_kernel(scale, *refs),
+        out_shape=jax.ShapeDtypeStruct((Y, R, LANES), F32),
+        in_specs=[vmem, vmem, smem] + [vmem] * (Y + 1),
+        out_specs=vmem,
+        scratch_shapes=[pltpu.VMEM((LANES, LANES), F32)],
+        compiler_params=pltpu.CompilerParams(vmem_limit_bytes=32 * MIB),
+        cost_estimate=pl.CostEstimate(flops=10**9, bytes_accessed=3 * MIB, transcendentals=0),
         name="score",
-    )(parts, train, info, y, *queries)
+    )(tp, got, at, *queries)
 
 
 def body(x_act, g_out, proj_in, proj_out, queries, cand_ids, cand_counts):
     n_layers = lax.axis_size("block")
     my_y = lax.axis_index("y").astype(jnp.int32)
-    me = lax.axis_index("z").astype(jnp.int32) * Y + my_y
-    query = [queries[0]]
-    for k in range(1, Y):
-        query.append(lax.ppermute(queries[0], "y", [(y, (y + k) % Y) for y in range(Y)]))
+    my_z = lax.axis_index("z").astype(jnp.int32)
+    me = my_z * Y + my_y
+    up = [(y, (y + 1) % Y) for y in range(Y)]
+    down = [(y, (y - 1) % Y) for y in range(Y)]
+    below = lax.ppermute(queries[0], "y", up)
+    above = lax.ppermute(queries[0], "y", down)
     packet = project(
         x_act[0],
         g_out[0],
@@ -315,33 +336,34 @@
         cand_ids[0].T,
         cand_counts,
     )
-    got = lax.all_to_all(packet.astype(F16), "z", 0, 0, tiled=True)
+    packet = jnp.broadcast_to(packet.astype(F16)[None], (Z, PACK, LANES))
+    got = lax.all_to_all(packet, "z", 0, 0, tiled=True)
 
     r = jnp.arange(40)[:, None]
     lane = jnp.arange(LANES)[None, :]
     upper = (lane % R >= r + R // 2 * (lane // R)) & (r < 32)
     power = jnp.where(
         upper[None],
-        got[:, HIGH + 33 : HIGH + 34].astype(F32),
-        got[:, HIGH + 34 : HIGH + 35].astype(F32),
+        got[:, NOTES + 1 : NOTES + 2].astype(F32),
+        got[:, NOTES + 2 : NOTES + 3].astype(F32),
     )
-    both = got[:, HIGH:LOW].astype(F32) + got[:, LOW:NAMED].astype(F32) * (1.0 / 1024.0)
+    low = jnp.pad(got[:, LOW:].astype(F32), ((0, 0), (0, LOW - NOTES), (0, 0)))
+    both = got[:, HIGH:LOW].astype(F32) + low * (1.0 / 1024.0)
     sums = jnp.sum(both * (jnp.exp2(power) * (1.0 / 128.0)), axis=0)
-    spread = jnp.broadcast_to(sums[None], (Y,) + sums.shape)
-    spread, got = lax.optimization_barrier((spread, got))
-    parts = lax.all_to_all(spread, "y", 0, 0, tiled=True)
-
-    train = got[:, :128].astype(F32)
-    info = jnp.concatenate(
-        [
-            jnp.sum(got[:, NAMED:].astype(F32), axis=0),
-            jnp.sum(got[:, HIGH + 35 : HIGH + 43].astype(F32), axis=0),
-        ],
-        axis=0,
-    )
+    parts = [sums] + [
+        lax.ppermute(sums, "y", [(y, (y + k) % Y) for y in range(Y)]) for k in range(1, Y)
+    ]
+    sums, got, below, above = lax.optimization_barrier((sums, got, below, above))
+    half = queries.shape[1] // 2
+    across_low = lax.ppermute(below[:half], "y", up)
+    across_high = lax.ppermute(above[half:], "y", down)
+    query = [queries[0], below, across_low, across_high, above]
+
+    wide = got[:, :LOW].astype(F32)
     scale = 1.0 / float(R * R * n_layers) ** 0.5 / 4096.0
     tokens = ROWS * Z * Y
-    scores = score(parts, train, info, jnp.reshape(my_y, (1,)), query, tokens, scale)
+    precond = solve(parts, wide, tokens)
+    scores = score(precond, wide, jnp.stack([my_z, my_y]), query, scale)
     scores = scores.reshape(Y * n_layers, R // n_layers, LANES)
     return jnp.sum(lax.all_to_all(scores, ("y", "block"), 0, 0, tiled=True), axis=0)
 

time: 66.9 us -> 62.4 us (0.933)
  waiting for transfers between devices: 18.1 us -> 13.5 us
  blocking collectives: 14.4 us -> 15.5 us
  other arithmetic: 2.85 us -> 1.82 us
    all_to_all x2 -> x1, starting transfers between devices: 13.2 us -> 9.02 us  [body(): got = lax.all_to_all(packet, 'z', 0, 0, tiled=True)]
    ppermute x3 -> x7, starting transfers between devices: 5.06 us -> 8.73 us  [the longest x3 3.85 us: body(): lax.ppermute(sums, 'y', [(y, (y + k) % Y) for y in range(Y)])]
    ppermute x3 -> x7, waiting for transfers between devices: 5.45 us -> 1.8 us  [the longest x3 1.14 us: body(): lax.ppermute(sums, 'y', [(y, (y + k) % Y) for y in range(Y)])]
    all_to_all x1, blocking collectives: 14.4 us -> 15.5 us  [body(): lax.all_to_all(scores, ('y', 'block'), 0, 0, tiled=True)]
    convert_element_type x2, other arithmetic: 2.04 us -> 0.95 us  [the longest x1 0.9 us: body(): packet = jnp.broadcast_to(packet.astype(F16)[None], (Z, PACK, LANES))]
    all_to_all x2 -> x1, waiting for transfers between devices: 12.7 us -> 11.7 us  [body(): got = lax.all_to_all(packet, 'z', 0, 0, tiled=True)]
    pallas_call x2 -> x3, Pallas kernels: 12.2 us -> 12.5 us  [the longest x1 6.46 us: project(): pl.pallas_call(project_kernel, out_shape=jax.ShapeDtypeStruct((PACK, LANE...]
  transfers between devices with their start and end apart: 5 -> 8, of which waited for: 3 -> 4; matrix products, arithmetic and copies ran while one was open for 1% -> 1% of each run, Pallas kernels for 0% -> 7%
where the time goes in v3:
time: 62.4 us; the launch traced here: 62.1 us
  starting transfers between devices  17.8 us (29%)
  blocking collectives  15.5 us (25%)
  waiting for transfers between devices  13.5 us (22%)
  Pallas kernels  12.5 us (20%)
  other arithmetic  1.82 us (3%)
  local copies, waits for them, and re-layouts  0.87 us (1%)
    all_to_all x1, blocking collectives, body(): lax.all_to_all(scores, ('y', 'block'), 0, 0, tiled=True)  15.5 us
    all_to_all x1, waiting for transfers between devices, body(): got = lax.all_to_all(packet, 'z', 0, 0, tiled=True)  11.7 us
    all_to_all x1, starting transfers between devices, body(): got = lax.all_to_all(packet, 'z', 0, 0, tiled=True)  9.02 us
    pallas_call x1, Pallas kernels, project(): pl.pallas_call(project_kernel, out_shape=jax.ShapeDtypeStruct((PACK, LANE...  6.46 us
    pallas_call x1, Pallas kernels, solve(): pl.pallas_call(lambda *refs: solve_kernel(float(tokens), *refs), out_shap...  4.57 us
    ppermute x3, starting transfers between devices, body(): lax.ppermute(sums, 'y', [(y, (y + k) % Y) for y in range(Y)])  3.85 us
    ppermute x1, starting transfers between devices, body(): above = lax.ppermute(queries[0], 'y', down)  2.81 us
    ppermute x1, starting transfers between devices, body(): across_high = lax.ppermute(above[half:], 'y', down)  2.06 us
  transfers between devices with their start and end apart: 8, of which 4 were waited for; matrix products, arithmetic and copies ran while one was open for 1% of the time, Pallas kernels for 7%

profile of v3, /device:TPU:1, one launch (start us, length us, event | category | flops | bytes accessed | tf_op | source)
XLA Modules:
  0.0 62.1 jit_solution(3955997877989480446)
XLA Ops:
  0.0 6.5 %project.1 = f32[200,128]{1,0:T(8,128)} custom-call(bf16[512,4096]{1,0:T(8,128)(2,1)} %bitcast.22, bf16[512,4096]{1,0:T(8,128)(2,1)} %bitcast.23, bf16[64,4096]{1,0:T(8,128)(2,1)} %bitcast.24, bf16[64,4096]{1,0:T(8,128)(2,1)} %bitcast.25, s32[1]{0:T(128)} %bitcast.6.me_ref, s32[2,32]{1,0:T(2,128)} %bitcast.28, s32[1,32]{1,0:T(1,128)} %counts_ref.1), custom_call_target="tpu_custom_call" | custom-call | tf_op jit(solution)/shard_map/project/pallas_call | solution.py:149
  6.5 0.9 %convert_element_type.14 = f16[200,128]{1,0:T(8,128)(2,1)S(1)} convert(f32[200,128]{1,0:T(8,128)} %project.1) | non-fusion elementwise | flops 25600 | bytes 153600 | tf_op jit(solution)/shard_map/convert_element_type | solution.py:339
  7.4 0.8 %broadcast_in_dim.43 = f16[8,200,128]{2,1,0:T(8,128)(2,1)} broadcast(f16[200,128]{1,0:T(8,128)(2,1)S(1)} %convert_element_type.14), dimensions={1,2} | broadcast | bytes 460800 | tf_op jit(solution)/shard_map/broadcast_in_dim | solution.py:339
  8.2 9.0 %all-to-all-start = ((f16[8,200,128]{2,1,0:T(8,128)(2,1)}), f16[8,200,128]{2,1,0:T(8,128)(2,1)S(1)}, u32[]{:S(2)}, u32[]{:S(2)}) async-start(f16[8,200,128]{2,1,0:T(8,128)(2,1)} %broadcast_in_dim.43), calls=%async_computation | async-start | bytes 819200 | tf_op jit(solution)/shard_map/all_to_all | solution.py:340
  17.2 2.8 %collective-permute-start.4 = (bf16[64,4096]{1,0:T(8,128)(2,1)S(1)}, bf16[64,4096]{1,0:T(8,128)(2,1)S(1)}, u32[]{:S(2)}, u32[]{:S(2)}) collective-permute-start(bf16[64,4096]{1,0:T(8,128)(2,1)S(1)} %bitcast.19), channel_id=1, source_target_pairs={{0,24},{8,0},{16,8},{24,16},{1,25},{9,1},{17,9},{25,17},{2,26},{10... | collective-permute-start | bytes 1572872 | tf_op jit(solution)/shard_map/ppermute | solution.py:329
  20.0 0.0 collective-permute-start.3
  20.0 0.1 pad_add_fusion.refs_2_
  20.1 0.1 fusion
  20.2 11.7 %all-to-all-done = f16[8,200,128]{2,1,0:T(8,128)(2,1)S(1)} async-done(((f16[8,200,128]{2,1,0:T(8,128)(2,1)}), f16[8,200,128]{2,1,0:T(8,128)(2,1)S(1)}, u32[]{:S(2)}, u32[]{:S(2)}) %all-to-all-start) | async-done | bytes 409632 | tf_op jit(solution)/shard_map/all_to_all | solution.py:340
  32.0 0.1 multiply_reduce_fusion.refs_0_
  32.0 2.8 %collective-permute-start.2 = (f32[40,128]{1,0:T(8,128)S(1)}, f32[40,128]{1,0:T(8,128)S(1)}, u32[]{:S(2)}, u32[]{:S(2)}) collective-permute-start(f32[40,128]{1,0:T(8,128)S(1)} %multiply_reduce_fusion.refs_0_), channel_id=1, source_target_pairs={{0,24},{8,0},{16,8},{24,16},{1,25},{9,1},{17,9},{25,17},{2,26},{10... | collective-permute-start | bytes 61448 | tf_op jit(solution)/shard_map/ppermute | solution.py:354
  34.9 0.3 collective-permute-start.1
  35.2 0.7 %collective-permute-start = (f32[40,128]{1,0:T(8,128)S(1)}, f32[40,128]{1,0:T(8,128)S(1)}, u32[]{:S(2)}, u32[]{:S(2)}) collective-permute-start(f32[40,128]{1,0:T(8,128)S(1)} %multiply_reduce_fusion.refs_0_), channel_id=1, source_target_pairs={{0,8},{8,16},{16,24},{24,0},{1,9},{9,17},{17,25},{25,1},{2,10},{10... | collective-permute-start | bytes 61448 | tf_op jit(solution)/shard_map/ppermute | solution.py:354
  35.9 0.0 collective-permute-done.4.refs_7_
  35.9 0.0 collective-permute-done.3.refs_4_
  36.0 2.1 %collective-permute-start.6 = (bf16[32,4096]{1,0:T(8,128)(2,1)S(1)}, bf16[32,4096]{1,0:T(8,128)(2,1)S(1)}, u32[]{:S(2)}, u32[]{:S(2)}) collective-permute-start(bf16[32,4096]{1,0:T(8,128)(2,1)S(1)} %slice.27), channel_id=1, source_target_pairs={{0,24},{8,0},{16,8},{24,16},{1,25},{9,1},{17,9},{25,17},{2,26},{10... | collective-permute-start | bytes 786440 | tf_op jit(solution)/shard_map/ppermute | solution.py:359
  38.1 0.9 %collective-permute-done.1.refs_2_ = f32[40,128]{1,0:T(8,128)S(1)} collective-permute-done((f32[40,128]{1,0:T(8,128)S(1)}, f32[40,128]{1,0:T(8,128)S(1)}, u32[]{:S(2)}, u32[]{:S(2)}) %collective-permute-start.1) | collective-permute-done | bytes 20512 | tf_op jit(solution)/shard_map/ppermute | solution.py:354
  39.0 0.2 collective-permute-done.refs_1_
  39.2 4.6 %solve.1.refs_0_ = bf16[32,4096]{1,0:T(8,128)(2,1)S(1)} custom-call(f32[40,128]{1,0:T(8,128)S(1)} %multiply_reduce_fusion.refs_0_, f32[40,128]{1,0:T(8,128)S(1)} %collective-permute-done.refs_1_, f32[40,128]{1,0:T(8,128)S(1)} %collective-permute-done.1.refs_2_, f32[40,128]{1,0:T(8,128)S(1)} %collective-permute-done.2.refs_3_, ...), custom_call_target="tpu_custom_call" | custom-call | flops 4000000000 | bytes 2097152 | tf_op jit(solution)/shard_map/solve/pallas_call | solution.py:290
  43.8 0.0 collective-permute-done.6.refs_6_
  43.8 0.7 %collective-permute-done.5.refs_5_ = bf16[32,4096]{1,0:T(8,128)(2,1)S(1)} collective-permute-done((bf16[32,4096]{1,0:T(8,128)(2,1)S(1)}, bf16[32,4096]{1,0:T(8,128)(2,1)S(1)}, u32[]{:S(2)}, u32[]{:S(2)}) %collective-permute-start.5) | collective-permute-done | bytes 262176 | tf_op jit(solution)/shard_map/ppermute | solution.py:358
  44.5 1.5 %score.1 = f32[4,64,128]{2,1,0:T(8,128)S(1)} custom-call(bf16[32,4096]{1,0:T(8,128)(2,1)S(1)} %solve.1.refs_0_, f32[8,168,128]{2,1,0:T(8,128)S(1)} %slice_convert_fusion.refs_4_.refs_1_, s32[2]{0:T(128)S(1)} %pad_add_fusion.refs_2_, bf16[64,4096]{1,0:T(8,128)(2,1)S(1)} %bitcast.21, bf16[64,4096]{1,0:T(8,128)(2,1)S(1)} %collective-permute-done.3.refs_4_, ...), custom_call_target="tpu_custom_call" | custom-call | flops 1000000000 | bytes 3145728 | tf_op jit(solution)/shard_map/score/pallas_call | solution.py:309
  46.0 15.5 %all_to_all.10 = f32[32,8,128]{2,1,0:T(8,128)S(1)} all-to-all(f32[32,8,128]{2,1,0:T(8,128)S(1)} %bitcast.18), channel_id=1, replica_groups=mesh['z'=8,'y'=4,'block'=8] {'y','block'}, dimensions={0} | all-to-all | bytes 262144 | tf_op jit(solution)/shard_map/all_to_all | solution.py:368
  61.5 0.6 %reduce_sum.19 = f32[8,128]{1,0:T(8,128)} reduce(f32[32,8,128]{2,1,0:T(8,128)S(1)} %all_to_all.10, f32[]{:T(128)} %constant.57.clone.1), dimensions={0}, to_apply=%region_1.2 | reduce | flops 31744 | bytes 135172 | tf_op jit(solution)/shard_map/reduce_sum | solution.py:368
  (11 shorter events, 0.1 us)
Async XLA Ops:
  0.0 17.2 %copy-start = (bf16[1,64,4096]{2,1,0:T(8,128)(2,1)S(1)}, bf16[1,64,4096]{2,1,0:T(8,128)(2,1)}, u32[]{:S(2)}) copy-start(bf16[1,64,4096]{2,1,0:T(8,128)(2,1)} %param.11) | copy-start | bytes 1572868
  8.2 23.7 %all-to-all-start = ((f16[8,200,128]{2,1,0:T(8,128)(2,1)}), f16[8,200,128]{2,1,0:T(8,128)(2,1)S(1)}, u32[]{:S(2)}, u32[]{:S(2)}) async-start(f16[8,200,128]{2,1,0:T(8,128)(2,1)} %broadcast_in_dim.43), calls=%async_computation | async-start | bytes 819200 | tf_op jit(solution)/shard_map/all_to_all | solution.py:340
  17.2 18.7 %collective-permute-start.4 = (bf16[64,4096]{1,0:T(8,128)(2,1)S(1)}, bf16[64,4096]{1,0:T(8,128)(2,1)S(1)}, u32[]{:S(2)}, u32[]{:S(2)}) collective-permute-start(bf16[64,4096]{1,0:T(8,128)(2,1)S(1)} %bitcast.19), channel_id=1, source_target_pairs={{0,24},{8,0},{16,8},{24,16},{1,25},{9,1},{17,9},{25,17},{2,26},{10... | collective-permute-start | bytes 1572872 | tf_op jit(solution)/shard_map/ppermute | solution.py:329
  20.0 15.9 %collective-permute-start.3 = (bf16[64,4096]{1,0:T(8,128)(2,1)S(1)}, bf16[64,4096]{1,0:T(8,128)(2,1)S(1)}, u32[]{:S(2)}, u32[]{:S(2)}) collective-permute-start(bf16[64,4096]{1,0:T(8,128)(2,1)S(1)} %bitcast.20), channel_id=1, source_target_pairs={{0,8},{8,16},{16,24},{24,0},{1,9},{9,17},{17,25},{25,1},{2,10},{10... | collective-permute-start | bytes 1572872 | tf_op jit(solution)/shard_map/ppermute | solution.py:328
  32.0 6.0 %collective-permute-start.2 = (f32[40,128]{1,0:T(8,128)S(1)}, f32[40,128]{1,0:T(8,128)S(1)}, u32[]{:S(2)}, u32[]{:S(2)}) collective-permute-start(f32[40,128]{1,0:T(8,128)S(1)} %multiply_reduce_fusion.refs_0_), channel_id=1, source_target_pairs={{0,24},{8,0},{16,8},{24,16},{1,25},{9,1},{17,9},{25,17},{2,26},{10... | collective-permute-start | bytes 61448 | tf_op jit(solution)/shard_map/ppermute | solution.py:354
  34.9 4.2 %collective-permute-start.1 = (f32[40,128]{1,0:T(8,128)S(1)}, f32[40,128]{1,0:T(8,128)S(1)}, u32[]{:S(2)}, u32[]{:S(2)}) collective-permute-start(f32[40,128]{1,0:T(8,128)S(1)} %multiply_reduce_fusion.refs_0_), channel_id=1, source_target_pairs={{0,16},{8,24},{16,0},{24,8},{1,17},{9,25},{17,1},{25,9},{2,18},{10... | collective-permute-start | bytes 61448 | tf_op jit(solution)/shard_map/ppermute | solution.py:354
  35.2 4.0 %collective-permute-start = (f32[40,128]{1,0:T(8,128)S(1)}, f32[40,128]{1,0:T(8,128)S(1)}, u32[]{:S(2)}, u32[]{:S(2)}) collective-permute-start(f32[40,128]{1,0:T(8,128)S(1)} %multiply_reduce_fusion.refs_0_), channel_id=1, source_target_pairs={{0,8},{8,16},{16,24},{24,0},{1,9},{9,17},{17,25},{25,1},{2,10},{10... | collective-permute-start | bytes 61448 | tf_op jit(solution)/shard_map/ppermute | solution.py:354
  36.0 7.8 %collective-permute-start.6 = (bf16[32,4096]{1,0:T(8,128)(2,1)S(1)}, bf16[32,4096]{1,0:T(8,128)(2,1)S(1)}, u32[]{:S(2)}, u32[]{:S(2)}) collective-permute-start(bf16[32,4096]{1,0:T(8,128)(2,1)S(1)} %slice.27), channel_id=1, source_target_pairs={{0,24},{8,0},{16,8},{24,16},{1,25},{9,1},{17,9},{25,17},{2,26},{10... | collective-permute-start | bytes 786440 | tf_op jit(solution)/shard_map/ppermute | solution.py:359
  38.0 6.4 %collective-permute-start.5 = (bf16[32,4096]{1,0:T(8,128)(2,1)S(1)}, bf16[32,4096]{1,0:T(8,128)(2,1)S(1)}, u32[]{:S(2)}, u32[]{:S(2)}) collective-permute-start(bf16[32,4096]{1,0:T(8,128)(2,1)S(1)} %slice.26), channel_id=1, source_target_pairs={{0,8},{8,16},{16,24},{24,0},{1,9},{9,17},{17,25},{25,1},{2,10},{10... | collective-permute-start | bytes 786440 | tf_op jit(solution)/shard_map/ppermute | solution.py:358

commit v4 on v3

--- a/solution.py
+++ b/solution.py
@@ -27,8 +27,8 @@
 WIDTH = D // CHUNKS
 MIB = 1024 * 1024
 
-HIGH = 128
-NOTES = 160
+NOTES = 128
+HIGH = 136
 LOW = 168
 PACK = 200
 
@@ -138,8 +138,8 @@
     notes = jnp.zeros((8, LANES), F32)
     for i, line in enumerate([diag, power[4:5], power[5:6], powers, named.astype(F32)]):
         notes = jnp.where(rows == i, line, notes)
-    out_ref[HIGH:NOTES, :] = high
-    out_ref[NOTES:LOW, :] = notes
+    out_ref[NOTES:HIGH, :] = notes
+    out_ref[HIGH:LOW, :] = high
     out_ref[LOW:PACK, :] = (packed - high) * 1024.0
 
 
@@ -199,17 +199,42 @@
     return jnp.where(r == c, tall, 0.0)
 
 
-def solve_kernel(tokens, p0, p1, p2, p3, t_ref, tp, lh, ll, u):
+def precondition(t_ref, left, ah, al, lh, ll, u, tp_ref):
+    for z in range(Z):
+        th, tl = split(jnp.concatenate([t_ref[z, :R, :], t_ref[z, R : 2 * R, :]], axis=1))
+        p = dot(left, th, NN)
+        q = dot(left[: 2 * R], tl, NN)
+        high, low = split(p[:R] + ((p[R : 2 * R] + q[:R]) + (p[2 * R :] + q[R:])))
+        lh[z * R : (z + 1) * R, :] = high
+        ll[z * R : (z + 1) * R, :] = low
+    for c in range(2):
+        rows = slice(c * 256, (c + 1) * 256)
+        high = lh[rows, :]
+        p = dot(high, ah, NN) + (dot(ll[rows, :], ah, NN) + dot(high, al, NN))
+        for s in range(4):
+            for t in range(2):
+                pair = (c * 4 + s) * 2 + t
+                u[pair * R : (pair + 1) * R, :] = p[s * R : (s + 1) * R, t * 128 : (t + 1) * 128]
+    low_half = lane_iota(16) < R
+    for i in range(0, R, 2):
+        w0 = u[pl.ds(i, 16, stride=R), :]
+        w1 = u[pl.ds(i + 1, 16, stride=R), :]
+        cols = slice(i * R, (i + 2) * R)
+        tp_ref[0:16, cols] = jnp.where(low_half, w0, swap_halves(w1)).astype(BF16)
+        tp_ref[16:32, cols] = jnp.where(low_half, swap_halves(w0), w1).astype(BF16)
+
+
+def solve_kernel(tokens, p0, p1, p2, p3, t_ref, tp_ref, left_ref, ah_ref, al_ref, lh, ll, u):
     total = (p0[...] + p2[...]) + (p1[...] + p3[...])
     first = lane_iota(R) < R
     row, col = row_iota(R), lane_iota(R) % R
-    packed = total[:32]
+    packed = total[8:]
     moved = swap_halves(packed)
     mixed = jnp.concatenate(
         [jnp.where(first[:32], packed, moved), jnp.where(first[:32], moved, packed)], axis=0
     )
     turned = jnp.concatenate([mixed, mixed], axis=0).T[:R]
-    diag_g = total[32:33]
+    diag_g = total[0:1]
     moved = swap_halves(diag_g)
     diag_g = jnp.where(first[:1], diag_g, moved) + jnp.where(first[:1], moved, diag_g) * (1.0 / 1024.0)
     factor_a = jnp.where(col >= row, mixed, turned)
@@ -222,76 +247,29 @@
     damp = (DAMP / R) * jnp.where(first[:1], trace_a, trace_g) + 1e-06
     m = invert_pair(jnp.where(on_diag, m + damp, m))
     other = swap_halves(m)
-    ia = block_diagonal(jnp.where(first, m, other))
+    ah, al = split(block_diagonal(jnp.where(first, m, other)))
     ig = jnp.where(first, other, m)[:, :R]
-
     g0 = ig.astype(BF16)
     g1, g2 = split(ig - g0.astype(F32))
     left = jnp.concatenate([g0, g1, g2], axis=0)
-    for z in range(Z):
-        th, tl = split(jnp.concatenate([t_ref[z, :R, :], t_ref[z, R : 2 * R, :]], axis=1))
-        p = dot(left, th, NN)
-        q = dot(left[: 2 * R], tl, NN)
-        high, low = split(p[:R] + ((p[R : 2 * R] + q[:R]) + (p[2 * R :] + q[R:])))
-        lh[z * R : (z + 1) * R, :] = high
-        ll[z * R : (z + 1) * R, :] = low
-    ah, al = split(ia)
-    for c in range(2):
-        rows = slice(c * 256, (c + 1) * 256)
-        high = lh[rows, :]
-        p = dot(high, ah, NN) + (dot(ll[rows, :], ah, NN) + dot(high, al, NN))
-        for s in range(4):
-            for t in range(2):
-                pair = (c * 4 + s) * 2 + t
-                u[pair * R : (pair + 1) * R, :] = p[s * R : (s + 1) * R, t * 128 : (t + 1) * 128]
-    low_half = first[:16]
-    for i in range(0, R, 2):
-        w0 = u[pl.ds(i, 16, stride=R), :]
-        w1 = u[pl.ds(i + 1, 16, stride=R), :]
-        cols = slice(i * R, (i + 2) * R)
-        tp[0:16, cols] = jnp.where(low_half, w0, swap_halves(w1)).astype(BF16)
-        tp[16:32, cols] = jnp.where(low_half, swap_halves(w0), w1).astype(BF16)
-
-
-def score_kernel(scale, tp, got_ref, at_ref, *refs):
-    queries, out_ref, names = refs[: Y + 1], *refs[Y + 1 :]
-    my_z, my_y = at_ref[0], at_ref[1]
-    s = jnp.concatenate([dot(queries[k][...], tp[...], NT) for k in range(Y + 1)], axis=0)
-    take = row_iota(32)
-    place = take % 16 // 2 * (Y * E_DEV) + my_y * E_DEV + take % 2 * 2 + take // 16
-    onehot = jnp.where(place == lane_iota(32), 1.0, 0.0).astype(BF16)
-    s0 = s.astype(BF16)
-    s1, s2 = split(s - s0.astype(F32))
-    s = dot(s0, onehot, NN) + (dot(s1, onehot, NN) + dot(s2, onehot, NN))
-    lanes = lane_iota(2 * Z)
-    mine = (lanes // (Y * E_DEV) == row_iota(2 * Z)) & (lanes // E_DEV % Y == my_y)
-    power = jnp.zeros((1, LANES), F32)
-    listed = []
-    for z in range(Z):
-        power = power + got_ref[z, NOTES + 3 : NOTES + 4, :]
-        listed.append(got_ref[z, NOTES + 4 : NOTES + 5, :])
-    listed = jnp.concatenate(listed + [jnp.zeros((Z, LANES), F32)], axis=0).astype(BF16)
-    names[...] = dot(listed, jnp.where(mine, 1.0, 0.0).astype(BF16), TN)
-    named = names[pl.ds(pl.multiple_of(my_z * (Y * CAP), Y * CAP), Y * CAP), :]
-    column = jnp.exp2(power) * scale
-    blocks = (row_iota(R) // QB).astype(F32)
-    for k in range(Y):
-        owner = (my_y + Y - k) % Y
-        id0, id1 = named[0:1], named[1:2]
-        for y in range(1, Y):
-            id0 = jnp.where(owner == y, named[2 * y : 2 * y + 1], id0)
-            id1 = jnp.where(owner == y, named[2 * y + 1 : 2 * y + 2], id1)
-        live = (blocks == id0) | (blocks == id1)
-        out_ref[owner] = jnp.where(live, s[k * R : (k + 1) * R] * column, 0.0)
-
-
-def solve(parts, train, tokens):
+    left_ref[...] = left
+    ah_ref[...] = ah
+    al_ref[...] = al
+    precondition(t_ref, left, ah, al, lh, ll, u, tp_ref)
+
+
+def solve(parts, wide, tokens):
     vmem = pl.BlockSpec(memory_space=pltpu.VMEM)
     return pl.pallas_call(
         lambda *refs: solve_kernel(float(tokens), *refs),
-        out_shape=jax.ShapeDtypeStruct((Z * E_DEV, D), BF16),
+        out_shape=(
+            jax.ShapeDtypeStruct((Z * E_DEV, D), BF16),
+            jax.ShapeDtypeStruct((3 * R, R), BF16),
+            jax.ShapeDtypeStruct((4 * R, 4 * R), BF16),
+            jax.ShapeDtypeStruct((4 * R, 4 * R), BF16),
+        ),
         in_specs=[vmem] * (Y + 1),
-        out_specs=vmem,
+        out_specs=(vmem,) * 4,
         scratch_shapes=[
             pltpu.VMEM((Z * R, 256), BF16),
             pltpu.VMEM((Z * R, 256), BF16),
@@ -300,33 +278,78 @@
         compiler_params=pltpu.CompilerParams(vmem_limit_bytes=32 * MIB),
         cost_estimate=pl.CostEstimate(flops=4 * 10**9, bytes_accessed=2 * MIB, transcendentals=0),
         name="solve",
-    )(*parts, train)
-
-
-def score(tp, got, at, queries, scale):
+    )(*parts, wide)
+
+
+def score_kernel(
+    scale, tp, left_ref, ah_ref, al_ref, wide, far, at_ref, q0, q1, out_ref, lh, ll, u, tq, names
+):
+    my_z, my_y, far_y = at_ref[0], at_ref[1], at_ref[2]
+    precondition(far, left_ref[...], ah_ref[...], al_ref[...], lh, ll, u, tq)
+    lanes = lane_iota(2 * Z)
+    rows = row_iota(2 * Z)
+    source = jnp.where(rows < Z, my_y, far_y)
+    mine = (lanes // (Y * E_DEV) == rows % Z) & (lanes // E_DEV % Y == source)
+    power = jnp.zeros((1, LANES), F32)
+    listed = []
+    for ref in (wide, far):
+        for z in range(Z):
+            power = power + ref[z, NOTES + 3 : NOTES + 4, :]
+            listed.append(ref[z, NOTES + 4 : NOTES + 5, :])
+    listed = jnp.concatenate(listed, axis=0).astype(BF16)
+    names[...] = dot(listed, jnp.where(mine, 1.0, 0.0).astype(BF16), TN)
+    named = names[pl.ds(pl.multiple_of(my_z * (Y * CAP), Y * CAP), Y * CAP), :]
+    column = jnp.exp2(power) * scale
+
+    examples = jnp.concatenate([tp[...], tq[...]], axis=0)
+    s = jnp.concatenate([dot(q0[...], examples, NT), dot(q1[...], examples, NT)], axis=0)
+    take = row_iota(64)
+    y = jnp.where(take < 32, my_y, far_y)
+    take = take % 32
+    place = take % 16 // 2 * (Y * E_DEV) + y * E_DEV + take % 2 * 2 + take // 16
+    onehot = jnp.where(place == lane_iota(64), 1.0, 0.0).astype(BF16)
+    s0 = s.astype(BF16)
+    s1, s2 = split(s - s0.astype(F32))
+    s = dot(s0, onehot, NN) + (dot(s1, onehot, NN) + dot(s2, onehot, NN))
+    blocks = (row_iota(R) // QB).astype(F32)
+    for k in range(2):
+        owner = my_y if k == 0 else my_y + 1 - my_y % 2 * 2
+        id0, id1 = named[0:1], named[1:2]
+        for y in range(1, Y):
+            id0 = jnp.where(owner == y, named[2 * y : 2 * y + 1], id0)
+            id1 = jnp.where(owner == y, named[2 * y + 1 : 2 * y + 2], id1)
+        live = (blocks == id0) | (blocks == id1)
+        out_ref[owner % 2] = jnp.where(live, s[k * R : (k + 1) * R] * column, 0.0)
+
+
+def score(solved, wide, far, at, queries, scale):
     vmem = pl.BlockSpec(memory_space=pltpu.VMEM)
     smem = pl.BlockSpec(memory_space=pltpu.SMEM)
     return pl.pallas_call(
         lambda *refs: score_kernel(scale, *refs),
-        out_shape=jax.ShapeDtypeStruct((Y, R, LANES), F32),
-        in_specs=[vmem, vmem, smem] + [vmem] * (Y + 1),
+        out_shape=jax.ShapeDtypeStruct((2, R, LANES), F32),
+        in_specs=[vmem] * 6 + [smem] + [vmem] * 2,
         out_specs=vmem,
-        scratch_shapes=[pltpu.VMEM((LANES, LANES), F32)],
+        scratch_shapes=[
+            pltpu.VMEM((Z * R, 256), BF16),
+            pltpu.VMEM((Z * R, 256), BF16),
+            pltpu.VMEM((2 * Z * R, LANES), F32),
+            pltpu.VMEM((Z * E_DEV, D), BF16),
+            pltpu.VMEM((LANES, LANES), F32),
+        ],
         compiler_params=pltpu.CompilerParams(vmem_limit_bytes=32 * MIB),
         cost_estimate=pl.CostEstimate(flops=10**9, bytes_accessed=3 * MIB, transcendentals=0),
         name="score",
-    )(tp, got, at, *queries)
+    )(*solved, wide, far, at, *queries)
 
 
 def body(x_act, g_out, proj_in, proj_out, queries, cand_ids, cand_counts):
     n_layers = lax.axis_size("block")
-    my_y = lax.axis_index("y").astype(jnp.int32)
     my_z = lax.axis_index("z").astype(jnp.int32)
+    my_y = lax.axis_index(("yh", "yl")).astype(jnp.int32)
     me = my_z * Y + my_y
-    up = [(y, (y + 1) % Y) for y in range(Y)]
-    down = [(y, (y - 1) % Y) for y in range(Y)]
-    below = lax.ppermute(queries[0], "y", up)
-    above = lax.ppermute(queries[0], "y", down)
+    far_y = (my_y + 3 + my_y % 2 * 2) % Y
+    near = lax.ppermute(queries[0], "yl", [(0, 1), (1, 0)])
     packet = project(
         x_act[0],
         g_out[0],
@@ -339,38 +362,37 @@
     packet = jnp.broadcast_to(packet.astype(F16)[None], (Z, PACK, LANES))
     got = lax.all_to_all(packet, "z", 0, 0, tiled=True)
 
-    r = jnp.arange(40)[:, None]
+    r = jnp.arange(LOW - NOTES)[:, None] - (HIGH - NOTES)
     lane = jnp.arange(LANES)[None, :]
-    upper = (lane % R >= r + R // 2 * (lane // R)) & (r < 32)
+    upper = (lane % R >= r + R // 2 * (lane // R)) & (r >= 0)
     power = jnp.where(
         upper[None],
         got[:, NOTES + 1 : NOTES + 2].astype(F32),
         got[:, NOTES + 2 : NOTES + 3].astype(F32),
     )
-    low = jnp.pad(got[:, LOW:].astype(F32), ((0, 0), (0, LOW - NOTES), (0, 0)))
-    both = got[:, HIGH:LOW].astype(F32) + low * (1.0 / 1024.0)
+    low = jnp.pad(got[:, LOW:].astype(F32), ((0, 0), (HIGH - NOTES, 0), (0, 0)))
+    both = got[:, NOTES:LOW].astype(F32) + low * (1.0 / 1024.0)
     sums = jnp.sum(both * (jnp.exp2(power) * (1.0 / 128.0)), axis=0)
     parts = [sums] + [
-        lax.ppermute(sums, "y", [(y, (y + k) % Y) for y in range(Y)]) for k in range(1, Y)
+        lax.ppermute(sums, ("yh", "yl"), [(y, (y + k) % Y) for y in range(Y)]) for k in range(1, Y)
     ]
-    sums, got, below, above = lax.optimization_barrier((sums, got, below, above))
-    half = queries.shape[1] // 2
-    across_low = lax.ppermute(below[:half], "y", up)
-    across_high = lax.ppermute(above[half:], "y", down)
-    query = [queries[0], below, across_low, across_high, above]
-
-    wide = got[:, :LOW].astype(F32)
+    sums, got = lax.optimization_barrier((sums, got))
+    own = got[:, :HIGH]
+    far = lax.ppermute(own, ("yh", "yl"), [(0, 3), (3, 0), (1, 2), (2, 1)])
+
     scale = 1.0 / float(R * R * n_layers) ** 0.5 / 4096.0
-    tokens = ROWS * Z * Y
-    precond = solve(parts, wide, tokens)
-    scores = score(precond, wide, jnp.stack([my_z, my_y]), query, scale)
-    scores = scores.reshape(Y * n_layers, R // n_layers, LANES)
-    return jnp.sum(lax.all_to_all(scores, ("y", "block"), 0, 0, tiled=True), axis=0)
+    wide = own.astype(F32)
+    solved = solve(parts, wide, ROWS * Z * Y)
+    at = jnp.stack([my_z, my_y, far_y])
+    scores = score(solved, wide, far.astype(F32), at, [queries[0], near], scale)
+    scores = scores.reshape(2 * n_layers, R // n_layers, LANES)
+    return jnp.sum(lax.all_to_all(scores, ("yl", "block"), 0, 0, tiled=True), axis=0)
 
 
 def solution(mesh):
-    split_mesh = Mesh(mesh.devices.reshape(Z, Y, -1), ("z", "y", "block"))
-    shard = ("z", "y")
+    axes = ("z", "yh", "yl", "block")
+    split_mesh = Mesh(mesh.devices.reshape(Z, 2, 2, -1), axes)
+    shard = axes[:3]
     return jax.shard_map(
         body,
         mesh=split_mesh,
@@ -383,6 +405,6 @@
             P(shard, None, None),
             P(shard, None),
         ),
-        out_specs=P(("z", "y", "block"), None),
+        out_specs=P(axes, None),
         check_vma=False,
     )

time: 62.4 us -> 59.9 us (0.960)
  blocking collectives: 15.5 us -> 12.6 us
  starting transfers between devices: 17.8 us -> 16.3 us
  waiting for transfers between devices: 13.5 us -> 14.7 us
  Pallas kernels: 12.5 us -> 13.2 us
    all_to_all x1, blocking collectives: 15.5 us -> 12.6 us  [body(): lax.all_to_all(scores, ('yl', 'block'), 0, 0, tiled=True)]
    all_to_all x1, waiting for transfers between devices: 11.7 us -> 13.2 us  [body(): got = lax.all_to_all(packet, 'z', 0, 0, tiled=True)]
    ppermute x7 -> x5, starting transfers between devices: 8.73 us -> 7.31 us  [the longest x3 3.85 us: body(): lax.ppermute(sums, ('yh', 'yl'), [(y, (y + k) % Y) for y in range(Y)])]
    pallas_call x1, Pallas kernels: 1.51 us -> 2.17 us  [score(): pl.pallas_call(lambda *refs: score_kernel(scale, *refs), out_shape=jax.Sh...]
    ppermute x7 -> x5, waiting for transfers between devices: 1.8 us -> 1.56 us  [the longest x3 1.17 us: body(): lax.ppermute(sums, ('yh', 'yl'), [(y, (y + k) % Y) for y in range(Y)])]
  transfers between devices with their start and end apart: 8 -> 6, of which waited for: 4 -> 4; matrix products, arithmetic and copies ran while one was open for 1% -> 1% of each run, Pallas kernels for 7% -> 8%
where the time goes in v4:
time: 59.9 us; the launch traced here: 59.7 us
  starting transfers between devices  16.3 us (27%)
  waiting for transfers between devices  14.7 us (25%)
  Pallas kernels  13.2 us (22%)
  blocking collectives  12.6 us (21%)
  other arithmetic  1.87 us (3%)
  local copies, waits for them, and re-layouts  0.83 us (1%)
    all_to_all x1, waiting for transfers between devices, body(): got = lax.all_to_all(packet, 'z', 0, 0, tiled=True)  13.2 us
    all_to_all x1, blocking collectives, body(): lax.all_to_all(scores, ('yl', 'block'), 0, 0, tiled=True)  12.6 us
    all_to_all x1, starting transfers between devices, body(): got = lax.all_to_all(packet, 'z', 0, 0, tiled=True)  9.02 us
    pallas_call x1, Pallas kernels, project(): pl.pallas_call(project_kernel, out_shape=jax.ShapeDtypeStruct((PACK, LANE...  6.46 us
    pallas_call x1, Pallas kernels, solve(): pl.pallas_call(lambda *refs: solve_kernel(float(tokens), *refs), out_shap...  4.58 us
    ppermute x3, starting transfers between devices, body(): lax.ppermute(sums, ('yh', 'yl'), [(y, (y + k) % Y) for y in range(Y)])  3.85 us
    pallas_call x1, Pallas kernels, score(): pl.pallas_call(lambda *refs: score_kernel(scale, *refs), out_shape=jax.Sh...  2.17 us
    ppermute x1, starting transfers between devices, body(): far = lax.ppermute(own, ('yh', 'yl'), [(0, 3), (3, 0), (1, 2), (2, 1)])  2.07 us
  transfers between devices with their start and end apart: 6, of which 4 were waited for; matrix products, arithmetic and copies ran while one was open for 1% of the time, Pallas kernels for 8%

profile of v4, /device:TPU:1, one launch (start us, length us, event | category | flops | bytes accessed | tf_op | source)
XLA Modules:
  0.0 59.7 jit_solution(18231279324923441207)
XLA Ops:
  0.0 6.5 %project.1 = f32[200,128]{1,0:T(8,128)} custom-call(bf16[512,4096]{1,0:T(8,128)(2,1)} %bitcast.22, bf16[512,4096]{1,0:T(8,128)(2,1)} %bitcast.23, bf16[64,4096]{1,0:T(8,128)(2,1)} %bitcast.24, bf16[64,4096]{1,0:T(8,128)(2,1)} %bitcast.25, s32[1]{0:T(128)} %bitcast.6.me_ref, s32[2,32]{1,0:T(2,128)} %bitcast.28, s32[1,32]{1,0:T(1,128)} %counts_ref.1), custom_call_target="tpu_custom_call" | custom-call | tf_op jit(solution)/shard_map/project/pallas_call | solution.py:149
  6.5 0.9 %convert_element_type.17 = f16[200,128]{1,0:T(8,128)(2,1)S(1)} convert(f32[200,128]{1,0:T(8,128)} %project.1) | non-fusion elementwise | flops 25600 | bytes 153600 | tf_op jit(solution)/shard_map/convert_element_type | solution.py:362
  7.4 0.8 %broadcast_in_dim.43 = f16[8,200,128]{2,1,0:T(8,128)(2,1)} broadcast(f16[200,128]{1,0:T(8,128)(2,1)S(1)} %convert_element_type.17), dimensions={1,2} | broadcast | bytes 460800 | tf_op jit(solution)/shard_map/broadcast_in_dim | solution.py:362
  8.2 9.0 %all-to-all-start = ((f16[8,200,128]{2,1,0:T(8,128)(2,1)}), f16[8,200,128]{2,1,0:T(8,128)(2,1)S(1)}, u32[]{:S(2)}, u32[]{:S(2)}) async-start(f16[8,200,128]{2,1,0:T(8,128)(2,1)} %broadcast_in_dim.43), calls=%async_computation | async-start | bytes 819200 | tf_op jit(solution)/shard_map/all_to_all | solution.py:363
  17.2 0.0 copy-done
  17.2 1.4 %collective-permute-start.4 = (bf16[64,4096]{1,0:T(8,128)(2,1)S(1)}, bf16[64,4096]{1,0:T(8,128)(2,1)S(1)}, u32[]{:S(2)}, u32[]{:S(2)}) collective-permute-start(bf16[64,4096]{1,0:T(8,128)(2,1)S(1)} %bitcast.20), channel_id=1, source_target_pairs={{0,8},{8,0},{1,9},{9,1},{2,10},{10,2},{3,11},{11,3},{4,12},{12,4},... | collective-permute-start | bytes 1572872 | tf_op jit(solution)/shard_map/ppermute | solution.py:352
  18.6 0.1 pad_add_fusion.refs_6_
  18.7 0.1 fusion
  18.8 13.2 %all-to-all-done = f16[8,200,128]{2,1,0:T(8,128)(2,1)S(1)} async-done(((f16[8,200,128]{2,1,0:T(8,128)(2,1)}), f16[8,200,128]{2,1,0:T(8,128)(2,1)S(1)}, u32[]{:S(2)}, u32[]{:S(2)}) %all-to-all-start) | async-done | bytes 409632 | tf_op jit(solution)/shard_map/all_to_all | solution.py:363
  32.0 0.1 multiply_reduce_fusion.refs_0_
  32.0 2.8 %collective-permute-start.2 = (f32[40,128]{1,0:T(8,128)S(1)}, f32[40,128]{1,0:T(8,128)S(1)}, u32[]{:S(2)}, u32[]{:S(2)}) collective-permute-start(f32[40,128]{1,0:T(8,128)S(1)} %multiply_reduce_fusion.refs_0_), channel_id=1, source_target_pairs={{0,24},{8,0},{16,8},{24,16},{1,25},{9,1},{17,9},{25,17},{2,26},{10... | collective-permute-start | bytes 61448 | tf_op jit(solution)/shard_map/ppermute | solution.py:377
  34.9 0.3 collective-permute-start.1
  35.2 0.7 %collective-permute-start = (f32[40,128]{1,0:T(8,128)S(1)}, f32[40,128]{1,0:T(8,128)S(1)}, u32[]{:S(2)}, u32[]{:S(2)}) collective-permute-start(f32[40,128]{1,0:T(8,128)S(1)} %multiply_reduce_fusion.refs_0_), channel_id=1, source_target_pairs={{0,8},{8,16},{16,24},{24,0},{1,9},{9,17},{17,25},{25,1},{2,10},{10... | collective-permute-start | bytes 61448 | tf_op jit(solution)/shard_map/ppermute | solution.py:377
  35.9 0.1 fusion.2
  36.0 2.1 %collective-permute-start.3 = (f16[8,136,128]{2,1,0:T(8,128)(2,1)S(1)}, f16[8,136,128]{2,1,0:T(8,128)(2,1)S(1)}, u32[]{:S(2)}, u32[]{:S(2)}) collective-permute-start(f16[8,136,128]{2,1,0:T(8,128)(2,1)S(1)} %get-tuple-element.15), channel_id=1, source_target_pairs={{0,24},{24,0},{8,16},{16,8},{1,25},{25,1},{9,17},{17,9},{2,26},{26... | collective-permute-start | bytes 835592 | tf_op jit(solution)/shard_map/ppermute | solution.py:381
  38.1 0.0 collective-permute-done.2.refs_3_
  38.1 1.0 %collective-permute-done.1.refs_2_ = f32[40,128]{1,0:T(8,128)S(1)} collective-permute-done((f32[40,128]{1,0:T(8,128)S(1)}, f32[40,128]{1,0:T(8,128)S(1)}, u32[]{:S(2)}, u32[]{:S(2)}) %collective-permute-start.1) | collective-permute-done | bytes 20512 | tf_op jit(solution)/shard_map/ppermute | solution.py:377
  39.0 0.2 collective-permute-done.refs_1_
  39.2 4.6 %solve.1 = (bf16[32,4096]{1,0:T(8,128)(2,1)S(1)}, bf16[192,64]{1,0:T(8,128)(2,1)S(1)}, bf16[256,256]{1,0:T(8,128)(2,1)S(1)}, bf16[256,256]{1,0:T(8,128)(2,1)S(1)}) custom-call(f32[40,128]{1,0:T(8,128)S(1)} %multiply_reduce_fusion.refs_0_, f32[40,128]{1,0:T(8,128)S(1)} %collective-permute-done.refs_1_, f32[40,128]{1,0:T(8,128)S(1)} %collective-permute-done.1.refs_2_, ...), custom_call_target="tpu_custom_call" | custom-call | flops 4000000000 | bytes 2097152 | tf_op jit(solution)/shard_map/solve/pallas_call | solution.py:263
  43.8 0.4 collective-permute-done.3
  44.2 0.0 collective-permute-done.4.refs_8_
  44.3 2.2 %score.1 = f32[2,64,128]{2,1,0:T(8,128)S(1)} custom-call(bf16[32,4096]{1,0:T(8,128)(2,1)S(1)} %get-tuple-element.11.refs_0_, bf16[192,64]{1,0:T(8,128)(2,1)S(1)} %get-tuple-element.12.refs_1_, bf16[256,256]{1,0:T(8,128)(2,1)S(1)} %get-tuple-element.13.refs_2_, bf16[256,256]{1,0:T(8,128)(2,1)S(1)} %get-tuple-element.14.refs_3_, ...), custom_call_target="tpu_custom_call" | custom-call | flops 1000000000 | bytes 3145728 | tf_op jit(solution)/shard_map/score/pallas_call | solution.py:328
  46.4 12.6 %all_to_all.10 = f32[16,8,128]{2,1,0:T(8,128)S(1)} all-to-all(f32[16,8,128]{2,1,0:T(8,128)S(1)} %bitcast.19), channel_id=1, replica_groups=mesh['z'=8,'yh'=2,'yl'=2,'block'=8] {'yl','block'}, dimensions={0} | all-to-all | bytes 131072 | tf_op jit(solution)/shard_map/all_to_all | solution.py:389
  59.1 0.6 %reduce_sum.19 = f32[8,128]{1,0:T(8,128)} reduce(f32[16,8,128]{2,1,0:T(8,128)S(1)} %all_to_all.10, f32[]{:T(128)} %constant.84.clone.1), dimensions={0}, to_apply=%region_1.2 | reduce | flops 15360 | bytes 69636 | tf_op jit(solution)/shard_map/reduce_sum | solution.py:389
  (7 shorter events, 0.1 us)
Async XLA Ops:
  0.0 17.2 %copy-start = (bf16[1,64,4096]{2,1,0:T(8,128)(2,1)S(1)}, bf16[1,64,4096]{2,1,0:T(8,128)(2,1)}, u32[]{:S(2)}) copy-start(bf16[1,64,4096]{2,1,0:T(8,128)(2,1)} %param.11) | copy-start | bytes 1572868
  8.2 23.7 %all-to-all-start = ((f16[8,200,128]{2,1,0:T(8,128)(2,1)}), f16[8,200,128]{2,1,0:T(8,128)(2,1)S(1)}, u32[]{:S(2)}, u32[]{:S(2)}) async-start(f16[8,200,128]{2,1,0:T(8,128)(2,1)} %broadcast_in_dim.43), calls=%async_computation | async-start | bytes 819200 | tf_op jit(solution)/shard_map/all_to_all | solution.py:363
  17.2 27.0 %collective-permute-start.4 = (bf16[64,4096]{1,0:T(8,128)(2,1)S(1)}, bf16[64,4096]{1,0:T(8,128)(2,1)S(1)}, u32[]{:S(2)}, u32[]{:S(2)}) collective-permute-start(bf16[64,4096]{1,0:T(8,128)(2,1)S(1)} %bitcast.20), channel_id=1, source_target_pairs={{0,8},{8,0},{1,9},{9,1},{2,10},{10,2},{3,11},{11,3},{4,12},{12,4},... | collective-permute-start | bytes 1572872 | tf_op jit(solution)/shard_map/ppermute | solution.py:352
  32.0 6.0 %collective-permute-start.2 = (f32[40,128]{1,0:T(8,128)S(1)}, f32[40,128]{1,0:T(8,128)S(1)}, u32[]{:S(2)}, u32[]{:S(2)}) collective-permute-start(f32[40,128]{1,0:T(8,128)S(1)} %multiply_reduce_fusion.refs_0_), channel_id=1, source_target_pairs={{0,24},{8,0},{16,8},{24,16},{1,25},{9,1},{17,9},{25,17},{2,26},{10... | collective-permute-start | bytes 61448 | tf_op jit(solution)/shard_map/ppermute | solution.py:377
  34.9 4.2 %collective-permute-start.1 = (f32[40,128]{1,0:T(8,128)S(1)}, f32[40,128]{1,0:T(8,128)S(1)}, u32[]{:S(2)}, u32[]{:S(2)}) collective-permute-start(f32[40,128]{1,0:T(8,128)S(1)} %multiply_reduce_fusion.refs_0_), channel_id=1, source_target_pairs={{0,16},{8,24},{16,0},{24,8},{1,17},{9,25},{17,1},{25,9},{2,18},{10... | collective-permute-start | bytes 61448 | tf_op jit(solution)/shard_map/ppermute | solution.py:377
  35.2 4.0 %collective-permute-start = (f32[40,128]{1,0:T(8,128)S(1)}, f32[40,128]{1,0:T(8,128)S(1)}, u32[]{:S(2)}, u32[]{:S(2)}) collective-permute-start(f32[40,128]{1,0:T(8,128)S(1)} %multiply_reduce_fusion.refs_0_), channel_id=1, source_target_pairs={{0,8},{8,16},{16,24},{24,0},{1,9},{9,17},{17,25},{25,1},{2,10},{10... | collective-permute-start | bytes 61448 | tf_op jit(solution)/shard_map/ppermute | solution.py:377
  36.0 8.2 %collective-permute-start.3 = (f16[8,136,128]{2,1,0:T(8,128)(2,1)S(1)}, f16[8,136,128]{2,1,0:T(8,128)(2,1)S(1)}, u32[]{:S(2)}, u32[]{:S(2)}) collective-permute-start(f16[8,136,128]{2,1,0:T(8,128)(2,1)S(1)} %get-tuple-element.15), channel_id=1, source_target_pairs={{0,24},{24,0},{8,16},{16,8},{1,25},{25,1},{9,17},{17,9},{2,26},{26... | collective-permute-start | bytes 835592 | tf_op jit(solution)/shard_map/ppermute | solution.py:381

commit v5 on v4

--- a/solution.py
+++ b/solution.py
@@ -25,6 +25,7 @@
 TN = (((0,), (0,)), ((), ()))
 CHUNKS = 8
 WIDTH = D // CHUNKS
+PANEL = 8
 MIB = 1024 * 1024
 
 NOTES = 128
@@ -148,7 +149,7 @@
     smem = pl.BlockSpec(memory_space=pltpu.SMEM)
     return pl.pallas_call(
         project_kernel,
-        out_shape=jax.ShapeDtypeStruct((PACK, LANES), F32),
+        out_shape=pltpu.VMEM((PACK, LANES), F32),
         in_specs=[hbm, hbm, hbm, hbm, smem, smem, smem],
         out_specs=pl.BlockSpec(memory_space=pltpu.VMEM),
         scratch_shapes=[
@@ -169,25 +170,41 @@
     rows = row_iota(R)
     half = jnp.where(lanes < R, 0, R)
     local = lane_iota(1) % R
-    for k in range(0, R, 2):
-        c0 = jnp.take_along_axis(m, half + k, axis=1)
-        c1 = jnp.take_along_axis(m, half + (k + 1), axis=1)
-        r0 = m[k : k + 1]
-        r1 = m[k + 1 : k + 2]
-        p00 = c0[k : k + 1]
-        p10 = c0[k + 1 : k + 2]
-        p01 = c1[k : k + 1]
-        p11 = c1[k + 1 : k + 2]
-        inv = 1.0 / (p00 * p11 - p01 * p10)
-        is0 = local == k
-        is1 = local == k + 1
-        r0 = jnp.where(is0, 1.0, jnp.where(is1, 0.0, r0))
-        r1 = jnp.where(is1, 1.0, jnp.where(is0, 0.0, r1))
-        q0 = (p11 * r0 - p01 * r1) * inv
-        q1 = (p00 * r1 - p10 * r0) * inv
-        kept = jnp.where(is0 | is1, 0.0, m)
-        m = kept - c0 * q0 - c1 * q1
-        m = jnp.where(rows == k, q0, jnp.where(rows == k + 1, q1, m))
+    for k in range(0, R, PANEL):
+        columns = [jnp.take_along_axis(m, half + (k + i), axis=1) for i in range(PANEL)]
+        lines = [m[k + i : k + i + 1] for i in range(PANEL)]
+        inside = (local >= k) & (local < k + PANEL)
+        steps = []
+        for j in range(0, PANEL, 2):
+            c0, c1 = columns[j], columns[j + 1]
+            a, b = k + j, k + j + 1
+            p00, p10 = c0[a : a + 1], c0[b : b + 1]
+            p01, p11 = c1[a : a + 1], c1[b : b + 1]
+            inv = 1.0 / (p00 * p11 - p01 * p10)
+            s00, s01, s10, s11 = p11 * inv, p01 * inv, p10 * inv, p00 * inv
+            is0, is1 = local == a, local == b
+            r0 = jnp.where(is0, 1.0, jnp.where(is1, 0.0, lines[j]))
+            r1 = jnp.where(is1, 1.0, jnp.where(is0, 0.0, lines[j + 1]))
+            q0 = s00 * r0 - s01 * r1
+            q1 = s11 * r1 - s10 * r0
+            for i in range(PANEL):
+                if i != j and i != j + 1:
+                    u0, u1 = c0[k + i : k + i + 1], c1[k + i : k + i + 1]
+                    lines[i] = jnp.where(is0 | is1, 0.0, lines[i]) - u0 * q0 - u1 * q1
+            lines[j], lines[j + 1] = q0, q1
+            for i in range(j + 2, PANEL):
+                x0, x1 = columns[i][a : a + 1], columns[i][b : b + 1]
+                y0 = s00 * x0 - s01 * x1
+                y1 = s11 * x1 - s10 * x0
+                column = columns[i] - c0 * y0 - c1 * y1
+                columns[i] = jnp.where(rows == a, y0, jnp.where(rows == b, y1, column))
+            steps = [(c, jnp.where(is0 | is1, 0.0, q)) for c, q in steps]
+            steps += [(c0, q0), (c1, q1)]
+        m = jnp.where(inside, 0.0, m)
+        for c, q in steps:
+            m = m - c * q
+        for i in range(PANEL):
+            m = jnp.where(rows == k + i, lines[i], m)
     return m
 
 

time: 59.9 us -> 58.2 us (0.972)
  Pallas kernels: 13.2 us -> 11.7 us
  waiting for transfers between devices: 14.7 us -> 15.6 us
  other arithmetic: 1.87 us -> 0.98 us
    pallas_call x1, Pallas kernels: 4.58 us -> 3.68 us  [solve(): pl.pallas_call(lambda *refs: solve_kernel(float(tokens), *refs), out_shap...]
    ppermute x1, waiting for transfers between devices: 0.4 us -> 1.3 us  [body(): far = lax.ppermute(own, ('yh', 'yl'), [(0, 3), (3, 0), (1, 2), (2, 1)])]
    convert_element_type x1, other arithmetic: 0.9 us -> 0.01 us  [body(): packet = jnp.broadcast_to(packet.astype(F16)[None], (Z, PACK, LANES))]
    pallas_call x1, Pallas kernels: 6.46 us -> 5.83 us  [project(): pl.pallas_call(project_kernel, out_shape=pltpu.VMEM((PACK, LANES), F32),...]
  transfers between devices with their start and end apart: 6 -> 6, of which waited for: 4 -> 4; matrix products, arithmetic and copies ran while one was open for 1% -> 1% of each run, Pallas kernels for 8% -> 6%
where the time goes in v5:
time: 58.2 us; the launch traced here: 58 us
  starting transfers between devices  16.3 us (28%)
  waiting for transfers between devices  15.6 us (27%)
  blocking collectives  12.5 us (21%)
  Pallas kernels  11.7 us (20%)
  other arithmetic  0.98 us (2%)
  local copies, waits for them, and re-layouts  0.83 us (1%)
    all_to_all x1, waiting for transfers between devices, body(): got = lax.all_to_all(packet, 'z', 0, 0, tiled=True)  13.2 us
    all_to_all x1, blocking collectives, body(): lax.all_to_all(scores, ('yl', 'block'), 0, 0, tiled=True)  12.5 us
    all_to_all x1, starting transfers between devices, body(): got = lax.all_to_all(packet, 'z', 0, 0, tiled=True)  9.02 us
    pallas_call x1, Pallas kernels, project(): pl.pallas_call(project_kernel, out_shape=pltpu.VMEM((PACK, LANES), F32),...  5.83 us
    ppermute x3, starting transfers between devices, body(): lax.ppermute(sums, ('yh', 'yl'), [(y, (y + k) % Y) for y in range(Y)])  3.85 us
    pallas_call x1, Pallas kernels, solve(): pl.pallas_call(lambda *refs: solve_kernel(float(tokens), *refs), out_shap...  3.68 us
    pallas_call x1, Pallas kernels, score(): pl.pallas_call(lambda *refs: score_kernel(scale, *refs), out_shape=jax.Sh...  2.16 us
    ppermute x1, starting transfers between devices, body(): far = lax.ppermute(own, ('yh', 'yl'), [(0, 3), (3, 0), (1, 2), (2, 1)])  2.07 us
  transfers between devices with their start and end apart: 6, of which 4 were waited for; matrix products, arithmetic and copies ran while one was open for 1% of the time, Pallas kernels for 6%

profile of v5, /device:TPU:1, one launch (start us, length us, event | category | flops | bytes accessed | tf_op | source)
XLA Modules:
  0.0 58.0 jit_solution(6792592449549390438)
XLA Ops:
  0.0 0.0 copy-start
  0.0 5.8 %project.1 = f32[200,128]{1,0:T(8,128)S(1)} custom-call(bf16[512,4096]{1,0:T(8,128)(2,1)} %bitcast.22, bf16[512,4096]{1,0:T(8,128)(2,1)} %bitcast.23, bf16[64,4096]{1,0:T(8,128)(2,1)} %bitcast.24, bf16[64,4096]{1,0:T(8,128)(2,1)} %bitcast.25, s32[1]{0:T(128)} %bitcast.6.me_ref, s32[2,32]{1,0:T(2,128)} %bitcast.28, s32[1,32]{1,0:T(1,128)} %counts_ref.1), custom_call_target="tpu_custom_call" | custom-call | tf_op jit(solution)/shard_map/project/pallas_call | solution.py:150
  5.9 0.8 %broadcast_in_dim.43 = f16[8,200,128]{2,1,0:T(8,128)(2,1)} broadcast(f16[200,128]{1,0:T(8,128)(2,1)S(1)} %convert_element_type.17), dimensions={1,2} | broadcast | bytes 460800 | tf_op jit(solution)/shard_map/broadcast_in_dim | solution.py:379
  6.7 9.0 %all-to-all-start = ((f16[8,200,128]{2,1,0:T(8,128)(2,1)}), f16[8,200,128]{2,1,0:T(8,128)(2,1)S(1)}, u32[]{:S(2)}, u32[]{:S(2)}) async-start(f16[8,200,128]{2,1,0:T(8,128)(2,1)} %broadcast_in_dim.43), calls=%async_computation | async-start | bytes 819200 | tf_op jit(solution)/shard_map/all_to_all | solution.py:380
  15.7 0.0 copy-done
  15.7 1.4 %collective-permute-start.4 = (bf16[64,4096]{1,0:T(8,128)(2,1)S(1)}, bf16[64,4096]{1,0:T(8,128)(2,1)S(1)}, u32[]{:S(2)}, u32[]{:S(2)}) collective-permute-start(bf16[64,4096]{1,0:T(8,128)(2,1)S(1)} %bitcast.20), channel_id=1, source_target_pairs={{0,8},{8,0},{1,9},{9,1},{2,10},{10,2},{3,11},{11,3},{4,12},{12,4},... | collective-permute-start | bytes 1572872 | tf_op jit(solution)/shard_map/ppermute | solution.py:369
  17.1 0.1 pad_add_fusion.refs_6_
  17.2 0.1 fusion
  17.2 13.2 %all-to-all-done = f16[8,200,128]{2,1,0:T(8,128)(2,1)S(1)} async-done(((f16[8,200,128]{2,1,0:T(8,128)(2,1)}), f16[8,200,128]{2,1,0:T(8,128)(2,1)S(1)}, u32[]{:S(2)}, u32[]{:S(2)}) %all-to-all-start) | async-done | bytes 409632 | tf_op jit(solution)/shard_map/all_to_all | solution.py:380
  30.4 0.1 multiply_reduce_fusion.refs_0_
  30.5 2.8 %collective-permute-start.2 = (f32[40,128]{1,0:T(8,128)S(1)}, f32[40,128]{1,0:T(8,128)S(1)}, u32[]{:S(2)}, u32[]{:S(2)}) collective-permute-start(f32[40,128]{1,0:T(8,128)S(1)} %multiply_reduce_fusion.refs_0_), channel_id=1, source_target_pairs={{0,24},{8,0},{16,8},{24,16},{1,25},{9,1},{17,9},{25,17},{2,26},{10... | collective-permute-start | bytes 61448 | tf_op jit(solution)/shard_map/ppermute | solution.py:394
  33.3 0.3 collective-permute-start.1
  33.7 0.7 %collective-permute-start = (f32[40,128]{1,0:T(8,128)S(1)}, f32[40,128]{1,0:T(8,128)S(1)}, u32[]{:S(2)}, u32[]{:S(2)}) collective-permute-start(f32[40,128]{1,0:T(8,128)S(1)} %multiply_reduce_fusion.refs_0_), channel_id=1, source_target_pairs={{0,8},{8,16},{16,24},{24,0},{1,9},{9,17},{17,25},{25,1},{2,10},{10... | collective-permute-start | bytes 61448 | tf_op jit(solution)/shard_map/ppermute | solution.py:394
  34.4 0.1 fusion.2
  34.5 2.1 %collective-permute-start.3 = (f16[8,136,128]{2,1,0:T(8,128)(2,1)S(1)}, f16[8,136,128]{2,1,0:T(8,128)(2,1)S(1)}, u32[]{:S(2)}, u32[]{:S(2)}) collective-permute-start(f16[8,136,128]{2,1,0:T(8,128)(2,1)S(1)} %get-tuple-element.15), channel_id=1, source_target_pairs={{0,24},{24,0},{8,16},{16,8},{1,25},{25,1},{9,17},{17,9},{2,26},{26... | collective-permute-start | bytes 835592 | tf_op jit(solution)/shard_map/ppermute | solution.py:398
  36.5 0.0 collective-permute-done.2.refs_3_
  36.5 1.0 %collective-permute-done.1.refs_2_ = f32[40,128]{1,0:T(8,128)S(1)} collective-permute-done((f32[40,128]{1,0:T(8,128)S(1)}, f32[40,128]{1,0:T(8,128)S(1)}, u32[]{:S(2)}, u32[]{:S(2)}) %collective-permute-start.1) | collective-permute-done | bytes 20512 | tf_op jit(solution)/shard_map/ppermute | solution.py:394
  37.5 0.2 collective-permute-done.refs_1_
  37.7 3.7 %solve.1 = (bf16[32,4096]{1,0:T(8,128)(2,1)S(1)}, bf16[192,64]{1,0:T(8,128)(2,1)S(1)}, bf16[256,256]{1,0:T(8,128)(2,1)S(1)}, bf16[256,256]{1,0:T(8,128)(2,1)S(1)}) custom-call(f32[40,128]{1,0:T(8,128)S(1)} %multiply_reduce_fusion.refs_0_, f32[40,128]{1,0:T(8,128)S(1)} %collective-permute-done.refs_1_, f32[40,128]{1,0:T(8,128)S(1)} %collective-permute-done.1.refs_2_, ...), custom_call_target="tpu_custom_call" | custom-call | flops 4000000000 | bytes 2097152 | tf_op jit(solution)/shard_map/solve/pallas_call | solution.py:280
  41.4 1.3 %collective-permute-done.3 = f16[8,136,128]{2,1,0:T(8,128)(2,1)S(1)} collective-permute-done((f16[8,136,128]{2,1,0:T(8,128)(2,1)S(1)}, f16[8,136,128]{2,1,0:T(8,128)(2,1)S(1)}, u32[]{:S(2)}, u32[]{:S(2)}) %collective-permute-start.3) | collective-permute-done | bytes 278560 | tf_op jit(solution)/shard_map/ppermute | solution.py:398
  42.7 0.0 collective-permute-done.4.refs_8_
  42.7 2.2 %score.1 = f32[2,64,128]{2,1,0:T(8,128)S(1)} custom-call(bf16[32,4096]{1,0:T(8,128)(2,1)S(1)} %get-tuple-element.11.refs_0_, bf16[192,64]{1,0:T(8,128)(2,1)S(1)} %get-tuple-element.12.refs_1_, bf16[256,256]{1,0:T(8,128)(2,1)S(1)} %get-tuple-element.13.refs_2_, bf16[256,256]{1,0:T(8,128)(2,1)S(1)} %get-tuple-element.14.refs_3_, ...), custom_call_target="tpu_custom_call" | custom-call | flops 1000000000 | bytes 3145728 | tf_op jit(solution)/shard_map/score/pallas_call | solution.py:345
  44.9 12.5 %all_to_all.10 = f32[16,8,128]{2,1,0:T(8,128)S(1)} all-to-all(f32[16,8,128]{2,1,0:T(8,128)S(1)} %bitcast.19), channel_id=1, replica_groups=mesh['z'=8,'yh'=2,'yl'=2,'block'=8] {'yl','block'}, dimensions={0} | all-to-all | bytes 131072 | tf_op jit(solution)/shard_map/all_to_all | solution.py:406
  57.4 0.6 %reduce_sum.19 = f32[8,128]{1,0:T(8,128)} reduce(f32[16,8,128]{2,1,0:T(8,128)S(1)} %all_to_all.10, f32[]{:T(128)} %constant.84.clone.1), dimensions={0}, to_apply=%region_1.2 | reduce | flops 15360 | bytes 69636 | tf_op jit(solution)/shard_map/reduce_sum | solution.py:406
  (7 shorter events, 0.1 us)
Async XLA Ops:
  0.0 15.7 %copy-start = (bf16[1,64,4096]{2,1,0:T(8,128)(2,1)S(1)}, bf16[1,64,4096]{2,1,0:T(8,128)(2,1)}, u32[]{:S(2)}) copy-start(bf16[1,64,4096]{2,1,0:T(8,128)(2,1)} %param.11) | copy-start | bytes 1572868
  6.7 23.7 %all-to-all-start = ((f16[8,200,128]{2,1,0:T(8,128)(2,1)}), f16[8,200,128]{2,1,0:T(8,128)(2,1)S(1)}, u32[]{:S(2)}, u32[]{:S(2)}) async-start(f16[8,200,128]{2,1,0:T(8,128)(2,1)} %broadcast_in_dim.43), calls=%async_computation | async-start | bytes 819200 | tf_op jit(solution)/shard_map/all_to_all | solution.py:380
  15.7 27.0 %collective-permute-start.4 = (bf16[64,4096]{1,0:T(8,128)(2,1)S(1)}, bf16[64,4096]{1,0:T(8,128)(2,1)S(1)}, u32[]{:S(2)}, u32[]{:S(2)}) collective-permute-start(bf16[64,4096]{1,0:T(8,128)(2,1)S(1)} %bitcast.20), channel_id=1, source_target_pairs={{0,8},{8,0},{1,9},{9,1},{2,10},{10,2},{3,11},{11,3},{4,12},{12,4},... | collective-permute-start | bytes 1572872 | tf_op jit(solution)/shard_map/ppermute | solution.py:369
  30.5 6.0 %collective-permute-start.2 = (f32[40,128]{1,0:T(8,128)S(1)}, f32[40,128]{1,0:T(8,128)S(1)}, u32[]{:S(2)}, u32[]{:S(2)}) collective-permute-start(f32[40,128]{1,0:T(8,128)S(1)} %multiply_reduce_fusion.refs_0_), channel_id=1, source_target_pairs={{0,24},{8,0},{16,8},{24,16},{1,25},{9,1},{17,9},{25,17},{2,26},{10... | collective-permute-start | bytes 61448 | tf_op jit(solution)/shard_map/ppermute | solution.py:394
  33.3 4.2 %collective-permute-start.1 = (f32[40,128]{1,0:T(8,128)S(1)}, f32[40,128]{1,0:T(8,128)S(1)}, u32[]{:S(2)}, u32[]{:S(2)}) collective-permute-start(f32[40,128]{1,0:T(8,128)S(1)} %multiply_reduce_fusion.refs_0_), channel_id=1, source_target_pairs={{0,16},{8,24},{16,0},{24,8},{1,17},{9,25},{17,1},{25,9},{2,18},{10... | collective-permute-start | bytes 61448 | tf_op jit(solution)/shard_map/ppermute | solution.py:394
  33.7 4.0 %collective-permute-start = (f32[40,128]{1,0:T(8,128)S(1)}, f32[40,128]{1,0:T(8,128)S(1)}, u32[]{:S(2)}, u32[]{:S(2)}) collective-permute-start(f32[40,128]{1,0:T(8,128)S(1)} %multiply_reduce_fusion.refs_0_), channel_id=1, source_target_pairs={{0,8},{8,16},{16,24},{24,0},{1,9},{9,17},{17,25},{25,1},{2,10},{10... | collective-permute-start | bytes 61448 | tf_op jit(solution)/shard_map/ppermute | solution.py:394
  34.5 8.2 %collective-permute-start.3 = (f16[8,136,128]{2,1,0:T(8,128)(2,1)S(1)}, f16[8,136,128]{2,1,0:T(8,128)(2,1)S(1)}, u32[]{:S(2)}, u32[]{:S(2)}) collective-permute-start(f16[8,136,128]{2,1,0:T(8,128)(2,1)S(1)} %get-tuple-element.15), channel_id=1, source_target_pairs={{0,24},{24,0},{8,16},{16,8},{1,25},{25,1},{9,17},{17,9},{2,26},{26... | collective-permute-start | bytes 835592 | tf_op jit(solution)/shard_map/ppermute | solution.py:398

commit v6 on v5

--- a/solution.py
+++ b/solution.py
@@ -51,7 +51,7 @@
 
 
 def exponent(m):
-    return jnp.clip(jnp.floor(jnp.log2(jnp.maximum(m, 1e-30))), -96.0, 96.0)
+    return jnp.clip(jnp.floor(jnp.log2(jnp.maximum(m, 1e-30))), -96.0, 126.0)
 
 
 def split(x):
@@ -241,7 +241,7 @@
         tp_ref[16:32, cols] = jnp.where(low_half, swap_halves(w0), w1).astype(BF16)
 
 
-def solve_kernel(tokens, p0, p1, p2, p3, t_ref, tp_ref, left_ref, ah_ref, al_ref, lh, ll, u):
+def solve_kernel(tokens, p0, p1, p2, p3, t_ref, tp_ref, left_ref, ah_ref, al_ref, power_ref, lh, ll, u):
     total = (p0[...] + p2[...]) + (p1[...] + p3[...])
     first = lane_iota(R) < R
     row, col = row_iota(R), lane_iota(R) % R
@@ -262,7 +262,11 @@
     trace_a = jnp.sum(jnp.where(first[:1], diag, 0.0), axis=1, keepdims=True)
     trace_g = jnp.sum(jnp.where(first[:1], 0.0, diag), axis=1, keepdims=True)
     damp = (DAMP / R) * jnp.where(first[:1], trace_a, trace_g) + 1e-06
-    m = invert_pair(jnp.where(on_diag, m + damp, m))
+    power_a = exponent(trace_a + R * damp[:, :1])
+    power_g = exponent(trace_g + R * damp[:, R : R + 1])
+    power_ref[...] = jnp.broadcast_to(power_a + power_g, (8, LANES))
+    shrink = jnp.exp2(-jnp.where(first[:1], power_a, power_g))
+    m = invert_pair(jnp.where(on_diag, m + damp, m) * shrink)
     other = swap_halves(m)
     ah, al = split(block_diagonal(jnp.where(first, m, other)))
     ig = jnp.where(first, other, m)[:, :R]
@@ -284,9 +288,10 @@
             jax.ShapeDtypeStruct((3 * R, R), BF16),
             jax.ShapeDtypeStruct((4 * R, 4 * R), BF16),
             jax.ShapeDtypeStruct((4 * R, 4 * R), BF16),
+            jax.ShapeDtypeStruct((8, LANES), F32),
         ),
         in_specs=[vmem] * (Y + 1),
-        out_specs=(vmem,) * 4,
+        out_specs=(vmem,) * 5,
         scratch_shapes=[
             pltpu.VMEM((Z * R, 256), BF16),
             pltpu.VMEM((Z * R, 256), BF16),
@@ -299,7 +304,7 @@
 
 
 def score_kernel(
-    scale, tp, left_ref, ah_ref, al_ref, wide, far, at_ref, q0, q1, out_ref, lh, ll, u, tq, names
+    scale, tp, left_ref, ah_ref, al_ref, power_ref, wide, far, at_ref, q0, q1, out_ref, lh, ll, u, tq, names
 ):
     my_z, my_y, far_y = at_ref[0], at_ref[1], at_ref[2]
     precondition(far, left_ref[...], ah_ref[...], al_ref[...], lh, ll, u, tq)
@@ -316,7 +321,7 @@
     listed = jnp.concatenate(listed, axis=0).astype(BF16)
     names[...] = dot(listed, jnp.where(mine, 1.0, 0.0).astype(BF16), TN)
     named = names[pl.ds(pl.multiple_of(my_z * (Y * CAP), Y * CAP), Y * CAP), :]
-    column = jnp.exp2(power) * scale
+    column = jnp.exp2(power - power_ref[0:1, :]) * scale
 
     examples = jnp.concatenate([tp[...], tq[...]], axis=0)
     s = jnp.concatenate([dot(q0[...], examples, NT), dot(q1[...], examples, NT)], axis=0)
@@ -345,7 +350,7 @@
     return pl.pallas_call(
         lambda *refs: score_kernel(scale, *refs),
         out_shape=jax.ShapeDtypeStruct((2, R, LANES), F32),
-        in_specs=[vmem] * 6 + [smem] + [vmem] * 2,
+        in_specs=[vmem] * 7 + [smem] + [vmem] * 2,
         out_specs=vmem,
         scratch_shapes=[
             pltpu.VMEM((Z * R, 256), BF16),

time: 58.2 us -> 58.2 us (level)
  no operation moved by 1% of the time
where the time goes in v6:
time: 58.2 us; the launch traced here: 58 us
  starting transfers between devices  16.3 us (28%)
  waiting for transfers between devices  15.6 us (27%)
  blocking collectives  12.5 us (21%)
  Pallas kernels  11.7 us (20%)
  other arithmetic  0.98 us (2%)
  local copies, waits for them, and re-layouts  0.83 us (1%)
    all_to_all x1, waiting for transfers between devices, body(): got = lax.all_to_all(packet, 'z', 0, 0, tiled=True)  13.2 us
    all_to_all x1, blocking collectives, body(): lax.all_to_all(scores, ('yl', 'block'), 0, 0, tiled=True)  12.5 us
    all_to_all x1, starting transfers between devices, body(): got = lax.all_to_all(packet, 'z', 0, 0, tiled=True)  9.02 us
    pallas_call x1, Pallas kernels, project(): pl.pallas_call(project_kernel, out_shape=pltpu.VMEM((PACK, LANES), F32),...  5.83 us
    ppermute x3, starting transfers between devices, body(): lax.ppermute(sums, ('yh', 'yl'), [(y, (y + k) % Y) for y in range(Y)])  3.85 us
    pallas_call x1, Pallas kernels, solve(): pl.pallas_call(lambda *refs: solve_kernel(float(tokens), *refs), out_shap...  3.75 us
    pallas_call x1, Pallas kernels, score(): pl.pallas_call(lambda *refs: score_kernel(scale, *refs), out_shape=jax.Sh...  2.16 us
    ppermute x1, starting transfers between devices, body(): far = lax.ppermute(own, ('yh', 'yl'), [(0, 3), (3, 0), (1, 2), (2, 1)])  2.07 us
  transfers between devices with their start and end apart: 6, of which 4 were waited for; matrix products, arithmetic and copies ran while one was open for 1% of the time, Pallas kernels for 6%

profile of v6, /device:TPU:1, one launch (start us, length us, event | category | flops | bytes accessed | tf_op | source)
XLA Modules:
  0.0 58.0 jit_solution(18301238537434486684)
XLA Ops:
  0.0 0.0 copy-start
  0.0 5.8 %project.1 = f32[200,128]{1,0:T(8,128)S(1)} custom-call(bf16[512,4096]{1,0:T(8,128)(2,1)} %bitcast.22, bf16[512,4096]{1,0:T(8,128)(2,1)} %bitcast.23, bf16[64,4096]{1,0:T(8,128)(2,1)} %bitcast.24, bf16[64,4096]{1,0:T(8,128)(2,1)} %bitcast.25, s32[1]{0:T(128)} %bitcast.6.me_ref, s32[2,32]{1,0:T(2,128)} %bitcast.28, s32[1,32]{1,0:T(1,128)} %counts_ref.1), custom_call_target="tpu_custom_call" | custom-call | tf_op jit(solution)/shard_map/project/pallas_call | solution.py:150
  5.9 0.8 %broadcast_in_dim.43 = f16[8,200,128]{2,1,0:T(8,128)(2,1)} broadcast(f16[200,128]{1,0:T(8,128)(2,1)S(1)} %convert_element_type.17), dimensions={1,2} | broadcast | bytes 460800 | tf_op jit(solution)/shard_map/broadcast_in_dim | solution.py:384
  6.7 9.0 %all-to-all-start = ((f16[8,200,128]{2,1,0:T(8,128)(2,1)}), f16[8,200,128]{2,1,0:T(8,128)(2,1)S(1)}, u32[]{:S(2)}, u32[]{:S(2)}) async-start(f16[8,200,128]{2,1,0:T(8,128)(2,1)} %broadcast_in_dim.43), calls=%async_computation | async-start | bytes 819200 | tf_op jit(solution)/shard_map/all_to_all | solution.py:385
  15.7 0.0 copy-done
  15.7 1.4 %collective-permute-start.4 = (bf16[64,4096]{1,0:T(8,128)(2,1)S(1)}, bf16[64,4096]{1,0:T(8,128)(2,1)S(1)}, u32[]{:S(2)}, u32[]{:S(2)}) collective-permute-start(bf16[64,4096]{1,0:T(8,128)(2,1)S(1)} %bitcast.20), channel_id=1, source_target_pairs={{0,8},{8,0},{1,9},{9,1},{2,10},{10,2},{3,11},{11,3},{4,12},{12,4},... | collective-permute-start | bytes 1572872 | tf_op jit(solution)/shard_map/ppermute | solution.py:374
  17.1 0.1 pad_add_fusion.refs_7_
  17.2 0.1 fusion
  17.2 13.2 %all-to-all-done = f16[8,200,128]{2,1,0:T(8,128)(2,1)S(1)} async-done(((f16[8,200,128]{2,1,0:T(8,128)(2,1)}), f16[8,200,128]{2,1,0:T(8,128)(2,1)S(1)}, u32[]{:S(2)}, u32[]{:S(2)}) %all-to-all-start) | async-done | bytes 409632 | tf_op jit(solution)/shard_map/all_to_all | solution.py:385
  30.4 0.1 multiply_reduce_fusion.refs_0_
  30.5 2.8 %collective-permute-start.2 = (f32[40,128]{1,0:T(8,128)S(1)}, f32[40,128]{1,0:T(8,128)S(1)}, u32[]{:S(2)}, u32[]{:S(2)}) collective-permute-start(f32[40,128]{1,0:T(8,128)S(1)} %multiply_reduce_fusion.refs_0_), channel_id=1, source_target_pairs={{0,24},{8,0},{16,8},{24,16},{1,25},{9,1},{17,9},{25,17},{2,26},{10... | collective-permute-start | bytes 61448 | tf_op jit(solution)/shard_map/ppermute | solution.py:399
  33.3 0.3 collective-permute-start.1
  33.7 0.7 %collective-permute-start = (f32[40,128]{1,0:T(8,128)S(1)}, f32[40,128]{1,0:T(8,128)S(1)}, u32[]{:S(2)}, u32[]{:S(2)}) collective-permute-start(f32[40,128]{1,0:T(8,128)S(1)} %multiply_reduce_fusion.refs_0_), channel_id=1, source_target_pairs={{0,8},{8,16},{16,24},{24,0},{1,9},{9,17},{17,25},{25,1},{2,10},{10... | collective-permute-start | bytes 61448 | tf_op jit(solution)/shard_map/ppermute | solution.py:399
  34.4 0.1 fusion.2
  34.5 2.1 %collective-permute-start.3 = (f16[8,136,128]{2,1,0:T(8,128)(2,1)S(1)}, f16[8,136,128]{2,1,0:T(8,128)(2,1)S(1)}, u32[]{:S(2)}, u32[]{:S(2)}) collective-permute-start(f16[8,136,128]{2,1,0:T(8,128)(2,1)S(1)} %get-tuple-element.17), channel_id=1, source_target_pairs={{0,24},{24,0},{8,16},{16,8},{1,25},{25,1},{9,17},{17,9},{2,26},{26... | collective-permute-start | bytes 835592 | tf_op jit(solution)/shard_map/ppermute | solution.py:403
  36.5 0.0 collective-permute-done.2.refs_3_
  36.5 1.0 %collective-permute-done.1.refs_2_ = f32[40,128]{1,0:T(8,128)S(1)} collective-permute-done((f32[40,128]{1,0:T(8,128)S(1)}, f32[40,128]{1,0:T(8,128)S(1)}, u32[]{:S(2)}, u32[]{:S(2)}) %collective-permute-start.1) | collective-permute-done | bytes 20512 | tf_op jit(solution)/shard_map/ppermute | solution.py:399
  37.5 0.2 collective-permute-done.refs_1_
  37.7 3.7 %solve.1 = (bf16[32,4096]{1,0:T(8,128)(2,1)S(1)}, bf16[192,64]{1,0:T(8,128)(2,1)S(1)}, bf16[256,256]{1,0:T(8,128)(2,1)S(1)}, bf16[256,256]{1,0:T(8,128)(2,1)S(1)}, f32[8,128]{1,0:T(8,128)S(1)}) custom-call(f32[40,128]{1,0:T(8,128)S(1)} %multiply_reduce_fusion.refs_0_, f32[40,128]{1,0:T(8,128)S(1)} %collective-permute-done.refs_1_, ...), custom_call_target="tpu_custom_call" | custom-call | flops 4000000000 | bytes 2097152 | tf_op jit(solution)/shard_map/solve/pallas_call | solution.py:284
  41.4 1.2 %collective-permute-done.3 = f16[8,136,128]{2,1,0:T(8,128)(2,1)S(1)} collective-permute-done((f16[8,136,128]{2,1,0:T(8,128)(2,1)S(1)}, f16[8,136,128]{2,1,0:T(8,128)(2,1)S(1)}, u32[]{:S(2)}, u32[]{:S(2)}) %collective-permute-start.3) | collective-permute-done | bytes 278560 | tf_op jit(solution)/shard_map/ppermute | solution.py:403
  42.7 0.0 collective-permute-done.4.refs_9_
  42.7 2.2 %score.1 = f32[2,64,128]{2,1,0:T(8,128)S(1)} custom-call(bf16[32,4096]{1,0:T(8,128)(2,1)S(1)} %get-tuple-element.12.refs_0_, bf16[192,64]{1,0:T(8,128)(2,1)S(1)} %get-tuple-element.13.refs_1_, bf16[256,256]{1,0:T(8,128)(2,1)S(1)} %get-tuple-element.14.refs_2_, bf16[256,256]{1,0:T(8,128)(2,1)S(1)} %get-tuple-element.15.refs_3_, ...), custom_call_target="tpu_custom_call" | custom-call | flops 1000000000 | bytes 3145728 | tf_op jit(solution)/shard_map/score/pallas_call | solution.py:350
  44.9 12.5 %all_to_all.10 = f32[16,8,128]{2,1,0:T(8,128)S(1)} all-to-all(f32[16,8,128]{2,1,0:T(8,128)S(1)} %bitcast.19), channel_id=1, replica_groups=mesh['z'=8,'yh'=2,'yl'=2,'block'=8] {'yl','block'}, dimensions={0} | all-to-all | bytes 131072 | tf_op jit(solution)/shard_map/all_to_all | solution.py:411
  57.4 0.6 %reduce_sum.19 = f32[8,128]{1,0:T(8,128)} reduce(f32[16,8,128]{2,1,0:T(8,128)S(1)} %all_to_all.10, f32[]{:T(128)} %constant.84.clone.1), dimensions={0}, to_apply=%region_1.2 | reduce | flops 15360 | bytes 69636 | tf_op jit(solution)/shard_map/reduce_sum | solution.py:411
  (7 shorter events, 0.1 us)
Async XLA Ops:
  0.0 15.7 %copy-start = (bf16[1,64,4096]{2,1,0:T(8,128)(2,1)S(1)}, bf16[1,64,4096]{2,1,0:T(8,128)(2,1)}, u32[]{:S(2)}) copy-start(bf16[1,64,4096]{2,1,0:T(8,128)(2,1)} %param.11) | copy-start | bytes 1572868
  6.7 23.7 %all-to-all-start = ((f16[8,200,128]{2,1,0:T(8,128)(2,1)}), f16[8,200,128]{2,1,0:T(8,128)(2,1)S(1)}, u32[]{:S(2)}, u32[]{:S(2)}) async-start(f16[8,200,128]{2,1,0:T(8,128)(2,1)} %broadcast_in_dim.43), calls=%async_computation | async-start | bytes 819200 | tf_op jit(solution)/shard_map/all_to_all | solution.py:385
  15.7 27.0 %collective-permute-start.4 = (bf16[64,4096]{1,0:T(8,128)(2,1)S(1)}, bf16[64,4096]{1,0:T(8,128)(2,1)S(1)}, u32[]{:S(2)}, u32[]{:S(2)}) collective-permute-start(bf16[64,4096]{1,0:T(8,128)(2,1)S(1)} %bitcast.20), channel_id=1, source_target_pairs={{0,8},{8,0},{1,9},{9,1},{2,10},{10,2},{3,11},{11,3},{4,12},{12,4},... | collective-permute-start | bytes 1572872 | tf_op jit(solution)/shard_map/ppermute | solution.py:374
  30.5 6.0 %collective-permute-start.2 = (f32[40,128]{1,0:T(8,128)S(1)}, f32[40,128]{1,0:T(8,128)S(1)}, u32[]{:S(2)}, u32[]{:S(2)}) collective-permute-start(f32[40,128]{1,0:T(8,128)S(1)} %multiply_reduce_fusion.refs_0_), channel_id=1, source_target_pairs={{0,24},{8,0},{16,8},{24,16},{1,25},{9,1},{17,9},{25,17},{2,26},{10... | collective-permute-start | bytes 61448 | tf_op jit(solution)/shard_map/ppermute | solution.py:399
  33.3 4.2 %collective-permute-start.1 = (f32[40,128]{1,0:T(8,128)S(1)}, f32[40,128]{1,0:T(8,128)S(1)}, u32[]{:S(2)}, u32[]{:S(2)}) collective-permute-start(f32[40,128]{1,0:T(8,128)S(1)} %multiply_reduce_fusion.refs_0_), channel_id=1, source_target_pairs={{0,16},{8,24},{16,0},{24,8},{1,17},{9,25},{17,1},{25,9},{2,18},{10... | collective-permute-start | bytes 61448 | tf_op jit(solution)/shard_map/ppermute | solution.py:399
  33.7 4.0 %collective-permute-start = (f32[40,128]{1,0:T(8,128)S(1)}, f32[40,128]{1,0:T(8,128)S(1)}, u32[]{:S(2)}, u32[]{:S(2)}) collective-permute-start(f32[40,128]{1,0:T(8,128)S(1)} %multiply_reduce_fusion.refs_0_), channel_id=1, source_target_pairs={{0,8},{8,16},{16,24},{24,0},{1,9},{9,17},{17,25},{25,1},{2,10},{10... | collective-permute-start | bytes 61448 | tf_op jit(solution)/shard_map/ppermute | solution.py:399
  34.5 8.2 %collective-permute-start.3 = (f16[8,136,128]{2,1,0:T(8,128)(2,1)S(1)}, f16[8,136,128]{2,1,0:T(8,128)(2,1)S(1)}, u32[]{:S(2)}, u32[]{:S(2)}) collective-permute-start(f16[8,136,128]{2,1,0:T(8,128)(2,1)S(1)} %get-tuple-element.17), channel_id=1, source_target_pairs={{0,24},{24,0},{8,16},{16,8},{1,25},{25,1},{9,17},{17,9},{2,26},{26... | collective-permute-start | bytes 835592 | tf_op jit(solution)/shard_map/ppermute | solution.py:403

commit v7 on v6

--- a/solution.py
+++ b/solution.py
@@ -23,8 +23,8 @@
 NT = (((1,), (1,)), ((), ()))
 NN = (((1,), (0,)), ((), ()))
 TN = (((0,), (0,)), ((), ()))
-CHUNKS = 8
-WIDTH = D // CHUNKS
+EDGES = [0, 512, 1024, 1536, 2048, 2560, 3072, 3584, 3840, D]
+CHUNKS = len(EDGES) - 1
 PANEL = 8
 MIB = 1024 * 1024
 
@@ -73,7 +73,7 @@
     pin_copy = fetch(pin_hbm, pin)
     x_copies, g_copies = [], []
     for c in range(CHUNKS):
-        cols = slice(c * WIDTH, (c + 1) * WIDTH)
+        cols = slice(EDGES[c], EDGES[c + 1])
         x_copies.append(fetch(x_hbm.at[:, cols], x.at[:, cols]))
         if c == 0:
             pout_copy = fetch(pout_hbm, pout)
@@ -88,7 +88,7 @@
 
     pin_copy.wait()
     for c in range(CHUNKS):
-        cols = slice(c * WIDTH, (c + 1) * WIDTH)
+        cols = slice(EDGES[c], EDGES[c + 1])
         x_copies[c].wait()
         xp = dot(pin[:, cols], x[:, cols], NT)
         if c == 0:
@@ -332,7 +332,8 @@
     onehot = jnp.where(place == lane_iota(64), 1.0, 0.0).astype(BF16)
     s0 = s.astype(BF16)
     s1, s2 = split(s - s0.astype(F32))
-    s = dot(s0, onehot, NN) + (dot(s1, onehot, NN) + dot(s2, onehot, NN))
+    s = dot(jnp.concatenate([s0, s1, s2], axis=0), onehot, NN)
+    s = s[: 2 * R] + (s[2 * R : 4 * R] + s[4 * R :])
     blocks = (row_iota(R) // QB).astype(F32)
     for k in range(2):
         owner = my_y if k == 0 else my_y + 1 - my_y % 2 * 2

time: 58.2 us -> 58.3 us (level)
  no operation moved by 1% of the time
where the time goes in v7:
time: 58.3 us; the launch traced here: 58.1 us
  starting transfers between devices  16.3 us (28%)
  waiting for transfers between devices  15.5 us (27%)
  blocking collectives  12.6 us (22%)
  Pallas kernels  11.8 us (20%)
  other arithmetic  0.98 us (2%)
  local copies, waits for them, and re-layouts  0.83 us (1%)
    all_to_all x1, waiting for transfers between devices, body(): got = lax.all_to_all(packet, 'z', 0, 0, tiled=True)  13.2 us
    all_to_all x1, blocking collectives, body(): lax.all_to_all(scores, ('yl', 'block'), 0, 0, tiled=True)  12.6 us
    all_to_all x1, starting transfers between devices, body(): got = lax.all_to_all(packet, 'z', 0, 0, tiled=True)  9.02 us
    pallas_call x1, Pallas kernels, project(): pl.pallas_call(project_kernel, out_shape=pltpu.VMEM((PACK, LANES), F32),...  5.87 us
    ppermute x3, starting transfers between devices, body(): lax.ppermute(sums, ('yh', 'yl'), [(y, (y + k) % Y) for y in range(Y)])  3.82 us
    pallas_call x1, Pallas kernels, solve(): pl.pallas_call(lambda *refs: solve_kernel(float(tokens), *refs), out_shap...  3.75 us
    pallas_call x1, Pallas kernels, score(): pl.pallas_call(lambda *refs: score_kernel(scale, *refs), out_shape=jax.Sh...  2.16 us
    ppermute x1, starting transfers between devices, body(): far = lax.ppermute(own, ('yh', 'yl'), [(0, 3), (3, 0), (1, 2), (2, 1)])  2.1 us
  transfers between devices with their start and end apart: 6, of which 4 were waited for; matrix products, arithmetic and copies ran while one was open for 1% of the time, Pallas kernels for 6%

profile of v7, /device:TPU:1, one launch (start us, length us, event | category | flops | bytes accessed | tf_op | source)
XLA Modules:
  0.0 58.1 jit_solution(14137539159707370559)
XLA Ops:
  0.0 0.0 copy-start
  0.0 5.9 %project.1 = f32[200,128]{1,0:T(8,128)S(1)} custom-call(bf16[512,4096]{1,0:T(8,128)(2,1)} %bitcast.22, bf16[512,4096]{1,0:T(8,128)(2,1)} %bitcast.23, bf16[64,4096]{1,0:T(8,128)(2,1)} %bitcast.24, bf16[64,4096]{1,0:T(8,128)(2,1)} %bitcast.25, s32[1]{0:T(128)} %bitcast.6.me_ref, s32[2,32]{1,0:T(2,128)} %bitcast.28, s32[1,32]{1,0:T(1,128)} %counts_ref.1), custom_call_target="tpu_custom_call" | custom-call | tf_op jit(solution)/shard_map/project/pallas_call | solution.py:150
  5.9 0.8 %broadcast_in_dim.43 = f16[8,200,128]{2,1,0:T(8,128)(2,1)} broadcast(f16[200,128]{1,0:T(8,128)(2,1)S(1)} %convert_element_type.17), dimensions={1,2} | broadcast | bytes 460800 | tf_op jit(solution)/shard_map/broadcast_in_dim | solution.py:385
  6.7 9.0 %all-to-all-start = ((f16[8,200,128]{2,1,0:T(8,128)(2,1)}), f16[8,200,128]{2,1,0:T(8,128)(2,1)S(1)}, u32[]{:S(2)}, u32[]{:S(2)}) async-start(f16[8,200,128]{2,1,0:T(8,128)(2,1)} %broadcast_in_dim.43), calls=%async_computation | async-start | bytes 819200 | tf_op jit(solution)/shard_map/all_to_all | solution.py:386
  15.7 0.0 copy-done
  15.7 1.4 %collective-permute-start.4 = (bf16[64,4096]{1,0:T(8,128)(2,1)S(1)}, bf16[64,4096]{1,0:T(8,128)(2,1)S(1)}, u32[]{:S(2)}, u32[]{:S(2)}) collective-permute-start(bf16[64,4096]{1,0:T(8,128)(2,1)S(1)} %bitcast.20), channel_id=1, source_target_pairs={{0,8},{8,0},{1,9},{9,1},{2,10},{10,2},{3,11},{11,3},{4,12},{12,4},... | collective-permute-start | bytes 1572872 | tf_op jit(solution)/shard_map/ppermute | solution.py:375
  17.1 0.1 pad_add_fusion.refs_7_
  17.2 0.1 fusion
  17.3 13.2 %all-to-all-done = f16[8,200,128]{2,1,0:T(8,128)(2,1)S(1)} async-done(((f16[8,200,128]{2,1,0:T(8,128)(2,1)}), f16[8,200,128]{2,1,0:T(8,128)(2,1)S(1)}, u32[]{:S(2)}, u32[]{:S(2)}) %all-to-all-start) | async-done | bytes 409632 | tf_op jit(solution)/shard_map/all_to_all | solution.py:386
  30.5 0.1 multiply_reduce_fusion.refs_0_
  30.6 2.8 %collective-permute-start.2 = (f32[40,128]{1,0:T(8,128)S(1)}, f32[40,128]{1,0:T(8,128)S(1)}, u32[]{:S(2)}, u32[]{:S(2)}) collective-permute-start(f32[40,128]{1,0:T(8,128)S(1)} %multiply_reduce_fusion.refs_0_), channel_id=1, source_target_pairs={{0,24},{8,0},{16,8},{24,16},{1,25},{9,1},{17,9},{25,17},{2,26},{10... | collective-permute-start | bytes 61448 | tf_op jit(solution)/shard_map/ppermute | solution.py:400
  33.4 0.4 collective-permute-start.1
  33.7 0.7 %collective-permute-start = (f32[40,128]{1,0:T(8,128)S(1)}, f32[40,128]{1,0:T(8,128)S(1)}, u32[]{:S(2)}, u32[]{:S(2)}) collective-permute-start(f32[40,128]{1,0:T(8,128)S(1)} %multiply_reduce_fusion.refs_0_), channel_id=1, source_target_pairs={{0,8},{8,16},{16,24},{24,0},{1,9},{9,17},{17,25},{25,1},{2,10},{10... | collective-permute-start | bytes 61448 | tf_op jit(solution)/shard_map/ppermute | solution.py:400
  34.4 0.1 fusion.2
  34.5 2.1 %collective-permute-start.3 = (f16[8,136,128]{2,1,0:T(8,128)(2,1)S(1)}, f16[8,136,128]{2,1,0:T(8,128)(2,1)S(1)}, u32[]{:S(2)}, u32[]{:S(2)}) collective-permute-start(f16[8,136,128]{2,1,0:T(8,128)(2,1)S(1)} %get-tuple-element.17), channel_id=1, source_target_pairs={{0,24},{24,0},{8,16},{16,8},{1,25},{25,1},{9,17},{17,9},{2,26},{26... | collective-permute-start | bytes 835592 | tf_op jit(solution)/shard_map/ppermute | solution.py:404
  36.6 0.0 collective-permute-done.2.refs_3_
  36.6 0.9 %collective-permute-done.1.refs_2_ = f32[40,128]{1,0:T(8,128)S(1)} collective-permute-done((f32[40,128]{1,0:T(8,128)S(1)}, f32[40,128]{1,0:T(8,128)S(1)}, u32[]{:S(2)}, u32[]{:S(2)}) %collective-permute-start.1) | collective-permute-done | bytes 20512 | tf_op jit(solution)/shard_map/ppermute | solution.py:400
  37.5 0.2 collective-permute-done.refs_1_
  37.7 3.8 %solve.1 = (bf16[32,4096]{1,0:T(8,128)(2,1)S(1)}, bf16[192,64]{1,0:T(8,128)(2,1)S(1)}, bf16[256,256]{1,0:T(8,128)(2,1)S(1)}, bf16[256,256]{1,0:T(8,128)(2,1)S(1)}, f32[8,128]{1,0:T(8,128)S(1)}) custom-call(f32[40,128]{1,0:T(8,128)S(1)} %multiply_reduce_fusion.refs_0_, f32[40,128]{1,0:T(8,128)S(1)} %collective-permute-done.refs_1_, ...), custom_call_target="tpu_custom_call" | custom-call | flops 4000000000 | bytes 2097152 | tf_op jit(solution)/shard_map/solve/pallas_call | solution.py:284
  41.5 1.2 %collective-permute-done.3 = f16[8,136,128]{2,1,0:T(8,128)(2,1)S(1)} collective-permute-done((f16[8,136,128]{2,1,0:T(8,128)(2,1)S(1)}, f16[8,136,128]{2,1,0:T(8,128)(2,1)S(1)}, u32[]{:S(2)}, u32[]{:S(2)}) %collective-permute-start.3) | collective-permute-done | bytes 278560 | tf_op jit(solution)/shard_map/ppermute | solution.py:404
  42.7 0.0 collective-permute-done.4.refs_9_
  42.7 2.2 %score.1 = f32[2,64,128]{2,1,0:T(8,128)S(1)} custom-call(bf16[32,4096]{1,0:T(8,128)(2,1)S(1)} %get-tuple-element.12.refs_0_, bf16[192,64]{1,0:T(8,128)(2,1)S(1)} %get-tuple-element.13.refs_1_, bf16[256,256]{1,0:T(8,128)(2,1)S(1)} %get-tuple-element.14.refs_2_, bf16[256,256]{1,0:T(8,128)(2,1)S(1)} %get-tuple-element.15.refs_3_, ...), custom_call_target="tpu_custom_call" | custom-call | flops 1000000000 | bytes 3145728 | tf_op jit(solution)/shard_map/score/pallas_call | solution.py:351
  44.9 12.6 %all_to_all.10 = f32[16,8,128]{2,1,0:T(8,128)S(1)} all-to-all(f32[16,8,128]{2,1,0:T(8,128)S(1)} %bitcast.19), channel_id=1, replica_groups=mesh['z'=8,'yh'=2,'yl'=2,'block'=8] {'yl','block'}, dimensions={0} | all-to-all | bytes 131072 | tf_op jit(solution)/shard_map/all_to_all | solution.py:412
  57.4 0.6 %reduce_sum.19 = f32[8,128]{1,0:T(8,128)} reduce(f32[16,8,128]{2,1,0:T(8,128)S(1)} %all_to_all.10, f32[]{:T(128)} %constant.84.clone.1), dimensions={0}, to_apply=%region_1.2 | reduce | flops 15360 | bytes 69636 | tf_op jit(solution)/shard_map/reduce_sum | solution.py:412
  (7 shorter events, 0.1 us)
Async XLA Ops:
  0.0 15.7 %copy-start = (bf16[1,64,4096]{2,1,0:T(8,128)(2,1)S(1)}, bf16[1,64,4096]{2,1,0:T(8,128)(2,1)}, u32[]{:S(2)}) copy-start(bf16[1,64,4096]{2,1,0:T(8,128)(2,1)} %param.11) | copy-start | bytes 1572868
  6.7 23.7 %all-to-all-start = ((f16[8,200,128]{2,1,0:T(8,128)(2,1)}), f16[8,200,128]{2,1,0:T(8,128)(2,1)S(1)}, u32[]{:S(2)}, u32[]{:S(2)}) async-start(f16[8,200,128]{2,1,0:T(8,128)(2,1)} %broadcast_in_dim.43), calls=%async_computation | async-start | bytes 819200 | tf_op jit(solution)/shard_map/all_to_all | solution.py:386
  15.7 27.0 %collective-permute-start.4 = (bf16[64,4096]{1,0:T(8,128)(2,1)S(1)}, bf16[64,4096]{1,0:T(8,128)(2,1)S(1)}, u32[]{:S(2)}, u32[]{:S(2)}) collective-permute-start(bf16[64,4096]{1,0:T(8,128)(2,1)S(1)} %bitcast.20), channel_id=1, source_target_pairs={{0,8},{8,0},{1,9},{9,1},{2,10},{10,2},{3,11},{11,3},{4,12},{12,4},... | collective-permute-start | bytes 1572872 | tf_op jit(solution)/shard_map/ppermute | solution.py:375
  30.6 6.0 %collective-permute-start.2 = (f32[40,128]{1,0:T(8,128)S(1)}, f32[40,128]{1,0:T(8,128)S(1)}, u32[]{:S(2)}, u32[]{:S(2)}) collective-permute-start(f32[40,128]{1,0:T(8,128)S(1)} %multiply_reduce_fusion.refs_0_), channel_id=1, source_target_pairs={{0,24},{8,0},{16,8},{24,16},{1,25},{9,1},{17,9},{25,17},{2,26},{10... | collective-permute-start | bytes 61448 | tf_op jit(solution)/shard_map/ppermute | solution.py:400
  33.4 4.1 %collective-permute-start.1 = (f32[40,128]{1,0:T(8,128)S(1)}, f32[40,128]{1,0:T(8,128)S(1)}, u32[]{:S(2)}, u32[]{:S(2)}) collective-permute-start(f32[40,128]{1,0:T(8,128)S(1)} %multiply_reduce_fusion.refs_0_), channel_id=1, source_target_pairs={{0,16},{8,24},{16,0},{24,8},{1,17},{9,25},{17,1},{25,9},{2,18},{10... | collective-permute-start | bytes 61448 | tf_op jit(solution)/shard_map/ppermute | solution.py:400
  33.7 4.0 %collective-permute-start = (f32[40,128]{1,0:T(8,128)S(1)}, f32[40,128]{1,0:T(8,128)S(1)}, u32[]{:S(2)}, u32[]{:S(2)}) collective-permute-start(f32[40,128]{1,0:T(8,128)S(1)} %multiply_reduce_fusion.refs_0_), channel_id=1, source_target_pairs={{0,8},{8,16},{16,24},{24,0},{1,9},{9,17},{17,25},{25,1},{2,10},{10... | collective-permute-start | bytes 61448 | tf_op jit(solution)/shard_map/ppermute | solution.py:400
  34.5 8.2 %collective-permute-start.3 = (f16[8,136,128]{2,1,0:T(8,128)(2,1)S(1)}, f16[8,136,128]{2,1,0:T(8,128)(2,1)S(1)}, u32[]{:S(2)}, u32[]{:S(2)}) collective-permute-start(f16[8,136,128]{2,1,0:T(8,128)(2,1)S(1)} %get-tuple-element.17), channel_id=1, source_target_pairs={{0,24},{24,0},{8,16},{16,8},{1,25},{25,1},{9,17},{17,9},{2,26},{26... | collective-permute-start | bytes 835592 | tf_op jit(solution)/shard_map/ppermute | solution.py:404
